TPU v7x, 128 devices: a whole 4x4x4 slice. The times are simulated.
128 devices in a mesh: grp: 2 (over z_hi), pix: 64 (over x, y, z_lo, core).
Axes of the slice: x: 4, y: 4, z: 4 (z_hi: 2, z_lo: 2; z = z_hi * 2 + z_lo), core: 2. Of those that a mesh axis runs over, the one named last changes fastest.
Arguments:
- fields: bfloat16 [2, 2, 128, 512, 512], P('grp', None, None, 'pix'), may hold values from -6 to 6
- lens_phase: float32 [512, 512], P('pix'), may hold values from -3.140625 to 3.140625
- occupancy: float32 [256], replicated, may hold values from 0.05 to 1
- focus_scale: float32 [256], replicated, may hold values from 0.5 to 1.5
- assignment: int32 [256], replicated, may hold values from 0 to 255, each once
- start_basis: float32 [2, 256, 128], replicated, may hold values from -6 to 6
Outputs:
- coherent_modes: bfloat16 [2, 128, 512, 512], P(None, None, 'pix', 'grp')
- relative_power: float32 [128], replicated
Inputs may be any that keep to these rules, and one draw needn't show every extreme that they name: `assignment`: each electron is carried by exactly one wavefront slot.
All inputs are finite; a program needn't handle non-finite values.
Results may differ from a plain program's by a relative error of at most 0.0018.
The roundings to bfloat16 on the way count: a program that leaves them out, or rounds other values in their place, can miss the bound.
Values may be sent and summed in bfloat16 or wider, within the bound.
No kernel may reach another device: no remote copies, remote signals or barrier semaphores. Data moves between devices by JAX's collectives and lax.ppermute only.
A program may use at most 64 MiB of HBM per device.

v0:
```python
import math

import jax
import jax.numpy as jnp
import numpy as np
from jax import lax
from jax.experimental import pallas as pl
from jax.experimental.pallas import tpu as pltpu
from jax.sharding import PartitionSpec as P

NROW = 512
NCOL = 512
STEPS = 2
GROUPS = 2
PIX = 64
DEVICES = GROUPS * PIX
SLOTS = 128
STACK = GROUPS * SLOTS
RANK = 128
ROWS = NROW // PIX
COLS = NCOL // DEVICES
HALF = NROW // GROUPS
WIDE = RANK * GROUPS * COLS
EARLY = 2
CHUNKS = 4
CHUNK = SLOTS // CHUNKS
BLOCK = DEVICES * 2 * ROWS
AXES = ("grp", "pix")

LIMIT = 0.5 * 1.5 * 3.140625


def fit(function, terms):
    limit = LIMIT * 1.001
    nodes = np.cos(np.pi * (np.arange(400) + 0.5) / 400)
    square = (nodes + 1.0) * 0.5 * limit * limit
    powers = np.stack([square**k for k in range(terms)], axis=1)
    return [float(c) for c in np.linalg.lstsq(powers, function(np.sqrt(square)), rcond=None)[0]]


SIN_FIT = fit(lambda x: np.sin(x) / x, 6)
COS_FIT = fit(np.cos, 7)


def tables(length):
    index = np.arange(length, dtype=np.int64)
    angle = (index[:, None] * index[None, :] % length).astype(np.float32) * np.float32(
        2.0 * math.pi / length
    )
    factor = np.float32(1.0 / math.sqrt(length))
    cosine = (np.cos(angle) * factor).astype(jnp.bfloat16)
    sine = (np.sin(angle) * factor).astype(jnp.bfloat16)
    return cosine, sine


def column_tables():
    i, g, p = np.meshgrid(np.arange(COLS), np.arange(GROUPS), np.arange(PIX), indexing="ij")
    order = (p * (GROUPS * COLS) + g * COLS + i).reshape(-1)
    cosine, sine = tables(NCOL)
    return cosine[order], sine[order]


def row_tables():
    cosine, sine = tables(NROW)
    cosine = cosine.reshape(NROW, PIX, ROWS)
    sine = sine.reshape(NROW, PIX, ROWS)
    real = np.stack([cosine, sine], axis=2).reshape(NROW, 2 * NROW)
    imag = np.stack([-sine, cosine], axis=2).reshape(NROW, 2 * NROW)
    return np.concatenate([real, imag], axis=0)


def polynomial(square, coefficients):
    total = square * coefficients[-1] + coefficients[-2]
    for coefficient in coefficients[-3::-1]:
        total = total * square + coefficient
    return total


def spectra_kernel(
    group_ref, assign_hbm, occ_hbm, chrom_hbm, fields_hbm, lens_hbm, cos_hbm, sin_hbm, out_hbm,
    assign_ref, occ_ref, chrom_ref, fields_ref, lens_ref, cos_ref, sin_ref,
    real_ref, imag_ref, wide_ref, out_ref, small_sem, field_sem, table_sem, out_sem,
):
    def chunk(part, c):
        slots = pl.ds(c * CHUNK, CHUNK)
        return pltpu.make_async_copy(
            fields_hbm.at[part, slots], fields_ref.at[part, slots], field_sem.at[part, c]
        )

    small = [
        pltpu.make_async_copy(source, target, small_sem.at[k])
        for k, (source, target) in enumerate(
            (
                (assign_hbm, assign_ref),
                (occ_hbm, occ_ref),
                (chrom_hbm, chrom_ref),
                (lens_hbm, lens_ref),
            )
        )
    ]
    large = [
        pltpu.make_async_copy(cos_hbm, cos_ref, table_sem.at[0]),
        pltpu.make_async_copy(sin_hbm, sin_ref, table_sem.at[1]),
    ]
    for copy in small:
        copy.start()
    for c in range(CHUNKS):
        for part in range(2):
            chunk(part, c).start()
    for copy in large:
        copy.start()
    for copy in small:
        copy.wait()
    base = group_ref[0] * SLOTS

    def phase(m, carry):
        electron = assign_ref[base + m]
        amplitude = jnp.sqrt(jnp.full((ROWS, 128), occ_ref[electron], jnp.float32))
        twice = amplitude + amplitude
        chromatic = chrom_ref[electron] * 0.5
        for lane in range(NCOL // 128):
            cut = pl.ds(lane * 128, 128)
            half = lens_ref[:, cut] * chromatic
            square = half * half
            sine_half = half * polynomial(square, SIN_FIT)
            scaled = sine_half * twice
            sine = scaled * polynomial(square, COS_FIT)
            cosine = amplitude - scaled * sine_half
            field_re = fields_ref[0, m, :, cut].astype(jnp.float32)
            field_im = fields_ref[1, m, :, cut].astype(jnp.float32)
            rows = pl.ds(pl.multiple_of(lane * ROWS * SLOTS + m * ROWS, ROWS), ROWS)
            real_ref[rows, :] = field_re * cosine - field_im * sine
            imag_ref[rows, :] = field_re * sine + field_im * cosine
        return carry

    for c in range(CHUNKS):
        for part in range(2):
            chunk(part, c).wait()
        lax.fori_loop(c * CHUNK, (c + 1) * CHUNK, phase, 0, unroll=4)
    for copy in large:
        copy.wait()
    contract = (((1,), (1,)), ((), ()))

    def product(table, wave):
        return lax.dot_general(table, wave, contract, preferred_element_type=jnp.float32)

    def wave(ref, j):
        return jnp.concatenate(
            [
                jnp.concatenate(
                    [
                        ref[pl.ds(lane * ROWS * SLOTS + j + q, SLOTS, stride=ROWS), :]
                        for lane in range(NCOL // 128)
                    ],
                    axis=1,
                )
                for q in range(2)
            ],
            axis=0,
        ).astype(jnp.bfloat16)

    cosine = cos_ref[...]
    sine = sin_ref[...]
    for j in range(0, ROWS, 2):
        wave_re = wave(real_ref, j)
        wave_im = wave(imag_ref, j)
        across_re = product(cosine, wave_re) + product(sine, wave_im)
        across_im = product(cosine, wave_im) - product(sine, wave_re)
        for part, across in ((0, across_re), (1, across_im)):
            for q in range(2):
                for i in range(COLS):
                    at = i * BLOCK + part * ROWS + j + q
                    wide_ref[pl.ds(at, DEVICES, stride=2 * ROWS), :] = across[
                        i * DEVICES : (i + 1) * DEVICES, q * SLOTS : (q + 1) * SLOTS
                    ]
    stores = []
    for i in range(COLS):
        out_ref[i] = (
            wide_ref[i * BLOCK : (i + 1) * BLOCK, :]
            .astype(jnp.bfloat16)
            .reshape(DEVICES, 2 * ROWS, SLOTS)
        )
        stores.append(pltpu.make_async_copy(out_ref.at[i], out_hbm.at[:, i], out_sem.at[i]))
        stores[-1].start()
    for copy in stores:
        copy.wait()


def focal_kernel(group_ref, pieces_ref, table_ref, keep_ref, early_ref, late_ref, gram_ref):
    group = group_ref[0]
    real = jnp.zeros((STACK, STACK), jnp.float32)
    cross = jnp.zeros((STACK, STACK), jnp.float32)
    for i in range(COLS):
        wave = jnp.concatenate(
            [
                pieces_ref[g * PIX : (g + 1) * PIX, i].reshape(2 * NROW, SLOTS)
                for g in range(GROUPS)
            ],
            axis=1,
        )
        focal = [
            jnp.dot(
                table_ref[part * NROW : (part + 1) * NROW, :],
                wave,
                preferred_element_type=jnp.float32,
            ).astype(jnp.bfloat16)
            for part in range(2)
        ]
        turned = [focal[part].T for part in range(2)]
        for part in range(2):
            low, high = turned[part][:, :HALF], turned[part][:, HALF:]
            keep_ref[part, i] = jnp.where(group == 0, low, high)
            sent = jnp.where(group == 0, high, low)
            if i < EARLY:
                early_ref[part, i] = sent
            else:
                late_ref[part, i - EARLY] = sent
        real += jnp.dot(turned[0], focal[0], preferred_element_type=jnp.float32)
        real += jnp.dot(turned[1], focal[1], preferred_element_type=jnp.float32)
        cross += jnp.dot(turned[0], focal[1], preferred_element_type=jnp.float32)
    imag = cross - cross.T
    row = lax.broadcasted_iota(jnp.int32, (STACK, STACK), 0)
    column = lax.broadcasted_iota(jnp.int32, (STACK, STACK), 1)
    packed = jnp.where(row <= column, real, imag)
    for q in range(4):
        top, left = (q // 2) * 128, (q % 2) * 128
        gram_ref[pl.ds(q, 128, stride=4), :] = packed[top : top + 128, left : left + 128]


def total_kernel(parts_ref, out_ref):
    total = jnp.sum(parts_ref[...].reshape(DEVICES // 2, 8, 128), axis=0)
    total = total[:4] + total[4:]
    twice = jnp.concatenate([total, total], axis=0)
    out_ref[...] = jnp.broadcast_to(twice[None], (DEVICES // 2, 8, 128)).reshape(4 * DEVICES, 128)


def power_kernel(gram_ref, start_ref, left_ref, scale_ref, power_ref):
    quads = [gram_ref[pl.ds(q, 128, stride=4), :] for q in range(4)]
    packed = jnp.concatenate(
        [jnp.concatenate(quads[:2], axis=1), jnp.concatenate(quads[2:], axis=1)], axis=0
    )
    turned = packed.T
    row = lax.broadcasted_iota(jnp.int32, (STACK, STACK), 0)
    column = lax.broadcasted_iota(jnp.int32, (STACK, STACK), 1)
    gram_re = jnp.where(row <= column, packed, turned)
    gram_im = jnp.where(row > column, packed, jnp.where(row == column, 0.0, -turned))
    gram = jnp.concatenate([gram_re, gram_im], axis=0)

    def apply(re, im):
        both = jnp.dot(
            gram,
            jnp.concatenate([re, im], axis=1),
            precision=lax.Precision.HIGHEST,
            preferred_element_type=jnp.float32,
        )
        return (
            both[:STACK, :RANK] - both[STACK:, RANK:],
            both[:STACK, RANK:] + both[STACK:, :RANK],
        )

    basis_re, basis_im = start_ref[0], start_ref[1]
    for _ in range(STEPS):
        image_re, image_im = apply(basis_re, basis_im)
        norm = jnp.sqrt(
            jnp.sum(image_re * image_re + image_im * image_im, axis=0, keepdims=True) + 1e-06
        )
        basis_re = image_re / norm
        basis_im = image_im / norm
    rounded_re = basis_re.astype(jnp.bfloat16).astype(jnp.float32)
    rounded_im = basis_im.astype(jnp.bfloat16).astype(jnp.float32)
    image_re, image_im = apply(rounded_re, rounded_im)
    energy = jnp.sum(rounded_re * image_re + rounded_im * image_im, axis=0, keepdims=True)
    trace = jnp.sum(jnp.where(row == column, packed, 0.0))
    power_ref[...] = energy * STACK / trace
    inverse = lax.rsqrt(energy / (NROW * NCOL) + 1e-06)
    scale_ref[...] = jnp.broadcast_to(inverse, (RANK, RANK)).T
    turned_re = rounded_re.T.astype(jnp.bfloat16)
    turned_im = rounded_im.T.astype(jnp.bfloat16)
    left_ref[:RANK, :STACK] = turned_re
    left_ref[:RANK, STACK:] = -turned_im
    left_ref[RANK:, :STACK] = turned_im
    left_ref[RANK:, STACK:] = turned_re


def modes_kernel(
    group_ref, left_ref, scale_ref, keep_ref, early_ref, late_ref, out_hbm,
    wide_ref, out_ref, out_sem,
):
    group = group_ref[0]
    left = left_ref[...]
    scale = scale_ref[...]
    for source in range(2):
        first = jnp.where(group == source, 0, COLS)
        for i in range(COLS):
            ref, at = keep_ref, i
            if source == 1:
                ref, at = (early_ref, i) if i < EARLY else (late_ref, i - EARLY)
            mode = jnp.dot(
                left, ref[:, at].reshape(2 * STACK, HALF), preferred_element_type=jnp.float32
            )
            for part in range(2):
                for lane in range(HALF // 128):
                    rows = pl.ds(
                        (part * 2 + lane) * WIDE + first + i, RANK, stride=GROUPS * COLS
                    )
                    wide_ref[rows, :] = (
                        mode[part * RANK : (part + 1) * RANK, lane * 128 : (lane + 1) * 128] * scale
                    )
    copies = []
    for part in range(2):
        for lane in range(HALF // 128):
            at = (part * 2 + lane) * WIDE
            out_ref[part, :, :, lane * 128 : (lane + 1) * 128] = (
                wide_ref[at : at + WIDE, :].reshape(RANK, GROUPS * COLS, 128).astype(jnp.bfloat16)
            )
        copies.append(pltpu.make_async_copy(out_ref.at[part], out_hbm.at[part], out_sem.at[part]))
        copies[-1].start()
    for copy in copies:
        copy.wait()


VMEM = pl.BlockSpec(memory_space=pltpu.VMEM)
HBM = pl.BlockSpec(memory_space=pltpu.HBM)
SMEM = pl.BlockSpec(memory_space=pltpu.SMEM)


def params(mib):
    return pltpu.CompilerParams(vmem_limit_bytes=mib * 1024 * 1024)


def local(fields, lens_phase, occupancy, focus_scale, assignment, start_basis):
    group = lax.axis_index("grp").astype(jnp.int32).reshape(1)
    cos_cols, sin_cols = (jnp.asarray(table) for table in column_tables())
    across = pl.pallas_call(
        spectra_kernel,
        out_shape=jax.ShapeDtypeStruct((DEVICES, COLS, 2 * ROWS, SLOTS), jnp.bfloat16),
        in_specs=[SMEM] + [HBM] * 7,
        out_specs=HBM,
        scratch_shapes=[
            pltpu.SMEM((STACK,), jnp.int32),
            pltpu.SMEM((STACK,), jnp.float32),
            pltpu.SMEM((STACK,), jnp.float32),
            pltpu.VMEM((2, SLOTS, ROWS, NCOL), jnp.bfloat16),
            pltpu.VMEM((ROWS, NCOL), jnp.float32),
            pltpu.VMEM((NCOL, NCOL), jnp.bfloat16),
            pltpu.VMEM((NCOL, NCOL), jnp.bfloat16),
            pltpu.VMEM((NCOL // 128 * ROWS * SLOTS, 128), jnp.float32),
            pltpu.VMEM((NCOL // 128 * ROWS * SLOTS, 128), jnp.float32),
            pltpu.VMEM((COLS * BLOCK, SLOTS), jnp.float32),
            pltpu.VMEM((COLS, DEVICES, 2 * ROWS, SLOTS), jnp.bfloat16),
            pltpu.SemaphoreType.DMA((4,)),
            pltpu.SemaphoreType.DMA((2, CHUNKS)),
            pltpu.SemaphoreType.DMA((2,)),
            pltpu.SemaphoreType.DMA((COLS,)),
        ],
        compiler_params=params(54),
        name="spectra",
    )(group, assignment, occupancy, focus_scale, fields[0], lens_phase, cos_cols, sin_cols)
    pieces = lax.all_to_all(across, AXES, 0, 0, tiled=True)

    def focal_shape(count):
        return jax.ShapeDtypeStruct((2, count, STACK, HALF), jnp.bfloat16)

    keep, early, late, gram = pl.pallas_call(
        focal_kernel,
        out_shape=(
            focal_shape(COLS),
            focal_shape(EARLY),
            focal_shape(COLS - EARLY),
            jax.ShapeDtypeStruct((4 * DEVICES, 128), jnp.float32),
        ),
        in_specs=[SMEM] + [VMEM] * 2,
        out_specs=(VMEM,) * 4,
        compiler_params=params(20),
        name="focal",
    )(group, pieces, jnp.asarray(row_tables()))
    early = lax.ppermute(early, "grp", [(0, 1), (1, 0)])
    late = lax.ppermute(late, "grp", [(0, 1), (1, 0)])
    parts = lax.all_to_all(gram.reshape(DEVICES, 4, 128), AXES, 0, 0, tiled=True)
    total = pl.pallas_call(
        total_kernel,
        out_shape=jax.ShapeDtypeStruct((4 * DEVICES, 128), jnp.float32),
        in_specs=[VMEM],
        out_specs=VMEM,
        compiler_params=params(4),
        name="total",
    )(parts.reshape(4 * DEVICES, 128))
    whole = lax.all_to_all(total.reshape(DEVICES, 4, 128), AXES, 0, 0, tiled=True)
    left, scale, power = pl.pallas_call(
        power_kernel,
        out_shape=(
            jax.ShapeDtypeStruct((2 * RANK, 2 * STACK), jnp.bfloat16),
            jax.ShapeDtypeStruct((RANK, RANK), jnp.float32),
            jax.ShapeDtypeStruct((1, RANK), jnp.float32),
        ),
        in_specs=[VMEM] * 2,
        out_specs=(VMEM,) * 3,
        compiler_params=params(12),
        name="power",
    )(whole.reshape(4 * DEVICES, 128), start_basis)
    coherent_modes = pl.pallas_call(
        modes_kernel,
        out_shape=jax.ShapeDtypeStruct((2, RANK, GROUPS * COLS, HALF), jnp.bfloat16),
        in_specs=[SMEM] + [VMEM] * 5,
        out_specs=HBM,
        scratch_shapes=[
            pltpu.VMEM((2 * HALF // 128 * WIDE, 128), jnp.float32),
            pltpu.VMEM((2, RANK, GROUPS * COLS, HALF), jnp.bfloat16),
            pltpu.SemaphoreType.DMA((2,)),
        ],
        compiler_params=params(16),
        name="modes",
    )(group, left, scale, keep, early, late)
    return coherent_modes, power.reshape(RANK)


def solution(mesh):
    in_specs = (P("grp", None, None, "pix", None), P("pix", None), P(), P(), P(), P())
    out_specs = (P(None, None, "pix", "grp"), P())

    return jax.shard_map(local, mesh=mesh, in_specs=in_specs, out_specs=out_specs, check_vma=False)
```

profile of v0, /device:TPU:1, one launch (start us, length us, event | category | flops | bytes accessed | tf_op | source)
XLA Modules:
  0.0 105.2 jit_solution(18096806945356035540)
XLA Ops:
  0.6 9.0 %spectra.1 = bf16[128,4,16,128]{3,2,1,0:T(8,128)(2,1)} custom-call(s32[1]{0:T(128)} %bitcast.group_ref, s32[256]{0:T(256)} %assign_hbm.1, f32[256]{0:T(256)} %occ_hbm.1, f32[256]{0:T(256)} %chrom_hbm.1, bf16[2,128,8,512]{3,2,1,0:T(8,128)(2,1)} %bitcast.11, f32[8,512]{1,0:T(8,128)} %lens_hbm.1, bf16[512,512]{1,0:T(8,128)(2,1)} %constant.12.clone.cos_hbm, ...), custom_call_target="tpu_custom_call" | custom-call | tf_op jit(solution)/shard_map/spectra/pallas_call | solution.py:334
  9.6 0.0 copy-start
  9.7 41.6 %all_to_all.15.pieces_ref = bf16[128,4,16,128]{3,2,1,0:T(8,128)(2,1)S(1)} all-to-all(bf16[128,4,16,128]{3,2,1,0:T(8,128)(2,1)} %spectra.1), channel_id=1, replica_groups=mesh['grp'=2,'pix'=64] {'grp','pix'}, dimensions={0} | all-to-all | bytes 4194304 | tf_op jit(solution)/shard_map/all_to_all | solution.py:359
  51.3 0.0 copy-done
  51.3 0.0 copy-start.1
  51.3 3.9 %focal.1 = (bf16[2,4,256,256]{3,2,1,0:T(8,128)(2,1)S(1)}, bf16[2,2,256,256]{3,2,1,0:T(8,128)(2,1)S(1)}, bf16[2,2,256,256]{3,2,1,0:T(8,128)(2,1)S(1)}, f32[512,128]{1,0:T(8,128)S(1)}) custom-call(s32[1]{0:T(128)} %bitcast.group_ref, bf16[128,4,16,128]{3,2,1,0:T(8,128)(2,1)S(1)} %all_to_all.15.pieces_ref, bf16[1024,1024]{1,0:T(8,128)(2,1)S(1)} %copy-done), custom_call_target="tpu_custom_call" | custom-call | tf_op jit(solution)/shard_map/focal/pallas_call | solution.py:364
  55.2 1.2 %collective-permute-start = (bf16[2,2,256,256]{3,2,1,0:T(8,128)(2,1)S(1)}, bf16[2,2,256,256]{3,2,1,0:T(8,128)(2,1)S(1)}, u32[]{:S(2)}, u32[]{:S(2)}) collective-permute-start(bf16[2,2,256,256]{3,2,1,0:T(8,128)(2,1)S(1)} %get-tuple-element.13), channel_id=1, source_target_pairs={{0,64},{64,0},{1,65},{65,1},{2,66},{66,2},{3,67},{67,3},{4,68},{68... | collective-permute-start | bytes 1572872 | tf_op jit(solution)/shard_map/ppermute | solution.py:377
  56.4 1.8 %collective-permute-start.1 = (bf16[2,2,256,256]{3,2,1,0:T(8,128)(2,1)S(1)}, bf16[2,2,256,256]{3,2,1,0:T(8,128)(2,1)S(1)}, u32[]{:S(2)}, u32[]{:S(2)}) collective-permute-start(bf16[2,2,256,256]{3,2,1,0:T(8,128)(2,1)S(1)} %get-tuple-element.14), channel_id=1, source_target_pairs={{0,64},{64,0},{1,65},{65,1},{2,66},{66,2},{3,67},{67,3},{4,68},{68... | collective-permute-start | bytes 1572872 | tf_op jit(solution)/shard_map/ppermute | solution.py:378
  58.3 26.6 %all_to_all.16 = f32[128,4,128]{2,1,0:T(4,128)S(1)} all-to-all(f32[128,4,128]{2,1,0:T(4,128)S(1)} %bitcast.10), channel_id=1, replica_groups=mesh['grp'=2,'pix'=64] {'grp','pix'}, dimensions={0} | all-to-all | bytes 524288 | tf_op jit(solution)/shard_map/all_to_all | solution.py:379
  84.8 0.1 total.1
  84.9 15.0 %all_to_all.17 = f32[128,4,128]{2,1,0:T(4,128)S(1)} all-to-all(f32[128,4,128]{2,1,0:T(4,128)S(1)} %bitcast.9), channel_id=1, replica_groups=mesh['grp'=2,'pix'=64] {'grp','pix'}, dimensions={0} | all-to-all | bytes 524288 | tf_op jit(solution)/shard_map/all_to_all | solution.py:388
  99.9 0.0 copy-done.1
  99.9 3.2 %power.1 = (bf16[256,512]{1,0:T(8,128)(2,1)S(1)}, f32[128,128]{1,0:T(8,128)S(1)}, f32[1,128]{1,0:T(1,128)}) custom-call(f32[512,128]{1,0:T(8,128)S(1)} %bitcast.7, f32[2,256,128]{2,1,0:T(8,128)S(1)} %copy-done.1), custom_call_target="tpu_custom_call" | custom-call | tf_op jit(solution)/shard_map/power/pallas_call | solution.py:389
  103.1 0.0 collective-permute-done.early_ref
  103.1 0.0 collective-permute-done.1.late_ref
  103.1 1.9 %modes.1 = bf16[2,128,8,256]{3,2,1,0:T(8,128)(2,1)} custom-call(s32[1]{0:T(128)} %bitcast.group_ref, bf16[256,512]{1,0:T(8,128)(2,1)S(1)} %get-tuple-element.10.left_ref, f32[128,128]{1,0:T(8,128)S(1)} %get-tuple-element.11.scale_ref, bf16[2,4,256,256]{3,2,1,0:T(8,128)(2,1)S(1)} %get-tuple-element.12.keep_ref, ...), custom_call_target="tpu_custom_call" | custom-call | tf_op jit(solution)/shard_map/modes/pallas_call | solution.py:401
Async XLA Ops:
  9.6 41.6 %copy-start = (bf16[1024,1024]{1,0:T(8,128)(2,1)S(1)}, bf16[1024,1024]{1,0:T(8,128)(2,1)}, u32[]{:S(2)}) copy-start(bf16[1024,1024]{1,0:T(8,128)(2,1)} %constant.14.clone.table_ref) | copy-start | bytes 6291460
  51.3 48.6 %copy-start.1 = (f32[2,256,128]{2,1,0:T(8,128)S(1)}, f32[2,256,128]{2,1,0:T(8,128)}, u32[]{:S(2)}) copy-start(f32[2,256,128]{2,1,0:T(8,128)} %start_ref.1) | copy-start | bytes 786436
  55.2 47.9 %collective-permute-start = (bf16[2,2,256,256]{3,2,1,0:T(8,128)(2,1)S(1)}, bf16[2,2,256,256]{3,2,1,0:T(8,128)(2,1)S(1)}, u32[]{:S(2)}, u32[]{:S(2)}) collective-permute-start(bf16[2,2,256,256]{3,2,1,0:T(8,128)(2,1)S(1)} %get-tuple-element.13), channel_id=1, source_target_pairs={{0,64},{64,0},{1,65},{65,1},{2,66},{66,2},{3,67},{67,3},{4,68},{68... | collective-permute-start | bytes 1572872 | tf_op jit(solution)/shard_map/ppermute | solution.py:377
  56.4 46.6 %collective-permute-start.1 = (bf16[2,2,256,256]{3,2,1,0:T(8,128)(2,1)S(1)}, bf16[2,2,256,256]{3,2,1,0:T(8,128)(2,1)S(1)}, u32[]{:S(2)}, u32[]{:S(2)}) collective-permute-start(bf16[2,2,256,256]{3,2,1,0:T(8,128)(2,1)S(1)} %get-tuple-element.14), channel_id=1, source_target_pairs={{0,64},{64,0},{1,65},{65,1},{2,66},{66,2},{3,67},{67,3},{4,68},{68... | collective-permute-start | bytes 1572872 | tf_op jit(solution)/shard_map/ppermute | solution.py:378
where the time goes:
time: 105 us
  blocking collectives  83.1 us (79%)
  Pallas kernels  18.1 us (17%)
  starting transfers between devices  3.05 us (3%)
    all_to_all x1, blocking collectives, local(): pieces = lax.all_to_all(across, AXES, 0, 0, tiled=True)  41.6 us
    all_to_all x1, blocking collectives, local(): lax.all_to_all(gram.reshape(DEVICES, 4, 128), AXES, 0, 0, tiled=True)  26.6 us
    all_to_all x1, blocking collectives, local(): lax.all_to_all(total.reshape(DEVICES, 4, 128), AXES, 0, 0, tiled=True)  15 us
    pallas_call x1, Pallas kernels, local(): pl.pallas_call(spectra_kernel, out_shape=jax.ShapeDtypeStruct((DEVICES, C...  9 us
    pallas_call x1, Pallas kernels, local(): pl.pallas_call(focal_kernel, out_shape=(focal_shape(COLS), focal_shape(EA...  3.94 us
    pallas_call x1, Pallas kernels, local(): pl.pallas_call(power_kernel, out_shape=(jax.ShapeDtypeStruct((2 * RANK, 2...  3.16 us
  transfers between devices with their start and end apart: 2, of which 0 were waited for; matrix products, arithmetic and copies ran while one was open for 0% of the time, Pallas kernels for 3%

commit v1 on v0

--- a/solution.py
+++ b/solution.py
@@ -21,7 +21,7 @@
 COLS = NCOL // DEVICES
 HALF = NROW // GROUPS
 WIDE = RANK * GROUPS * COLS
-EARLY = 2
+THIRD = 2
 CHUNKS = 4
 CHUNK = SLOTS // CHUNKS
 BLOCK = DEVICES * 2 * ROWS
@@ -54,19 +54,31 @@
 
 
 def column_tables():
-    i, g, p = np.meshgrid(np.arange(COLS), np.arange(GROUPS), np.arange(PIX), indexing="ij")
+    i, g, p = np.meshgrid(
+        np.arange(COLS), np.arange(GROUPS), np.arange(PIX // 2), indexing="ij"
+    )
     order = (p * (GROUPS * COLS) + g * COLS + i).reshape(-1)
-    cosine, sine = tables(NCOL)
-    return cosine[order], sine[order]
+    pair = np.arange(0, NCOL, 256)[:, None]
+    lane = np.arange(64)
+    even = np.concatenate([pair + 2 * lane, pair + 128 + 2 * lane], axis=1).reshape(-1)
+    odd = np.concatenate([pair + 129 + 2 * lane, pair + 1 + 2 * lane], axis=1).reshape(-1)
+    cosine, sine = (table[order] for table in tables(NCOL))
+    return np.stack(
+        [
+            np.block([[cosine[:, k], sine[:, k]], [-sine[:, k], cosine[:, k]]])
+            for k in (even, odd)
+        ]
+    )
 
 
 def row_tables():
-    cosine, sine = tables(NROW)
-    cosine = cosine.reshape(NROW, PIX, ROWS)
-    sine = sine.reshape(NROW, PIX, ROWS)
-    real = np.stack([cosine, sine], axis=2).reshape(NROW, 2 * NROW)
-    imag = np.stack([-sine, cosine], axis=2).reshape(NROW, 2 * NROW)
-    return np.concatenate([real, imag], axis=0)
+    cosine, sine = (
+        table[:HALF].reshape(HALF, PIX, ROWS // 2, 2).transpose(3, 0, 1, 2)
+        for table in tables(NROW)
+    )
+    real = np.stack([cosine, sine], axis=3).reshape(2, HALF, NROW)
+    imag = np.stack([-sine, cosine], axis=3).reshape(2, HALF, NROW)
+    return np.concatenate([real, imag], axis=1)
 
 
 def polynomial(square, coefficients):
@@ -77,8 +89,8 @@
 
 
 def spectra_kernel(
-    group_ref, assign_hbm, occ_hbm, chrom_hbm, fields_hbm, lens_hbm, cos_hbm, sin_hbm, out_hbm,
-    assign_ref, occ_ref, chrom_ref, fields_ref, lens_ref, cos_ref, sin_ref,
+    group_ref, assign_hbm, occ_hbm, chrom_hbm, fields_hbm, lens_hbm, table_hbm, out_hbm,
+    assign_ref, occ_ref, chrom_ref, fields_ref, lens_ref, table_ref,
     real_ref, imag_ref, wide_ref, out_ref, small_sem, field_sem, table_sem, out_sem,
 ):
     def chunk(part, c):
@@ -99,8 +111,8 @@
         )
     ]
     large = [
-        pltpu.make_async_copy(cos_hbm, cos_ref, table_sem.at[0]),
-        pltpu.make_async_copy(sin_hbm, sin_ref, table_sem.at[1]),
+        pltpu.make_async_copy(table_hbm.at[odd], table_ref.at[odd], table_sem.at[odd])
+        for odd in range(2)
     ]
     for copy in small:
         copy.start()
@@ -139,40 +151,49 @@
         lax.fori_loop(c * CHUNK, (c + 1) * CHUNK, phase, 0, unroll=4)
     for copy in large:
         copy.wait()
+    lane = lax.broadcasted_iota(jnp.int32, (SLOTS, 128), 1)
+    evens_first = 2 * (lane % 64) + lane // 64
+    odds_first = 2 * (lane % 64) + 1 - lane // 64
+
+    def parts(ref, j):
+        even, odd = [], []
+        for tile in range(0, NCOL // 128, 2):
+            left, right = (
+                ref[pl.ds((tile + k) * ROWS * SLOTS + j, SLOTS, stride=ROWS), :] for k in range(2)
+            )
+            left = jnp.take_along_axis(left, evens_first, axis=1)
+            right = jnp.take_along_axis(right, odds_first, axis=1)
+            even.append(jnp.where(lane < 64, left, right))
+            odd.append(jnp.where(lane < 64, right, left))
+        return even, odd
+
     contract = (((1,), (1,)), ((), ()))
-
-    def product(table, wave):
-        return lax.dot_general(table, wave, contract, preferred_element_type=jnp.float32)
-
-    def wave(ref, j):
-        return jnp.concatenate(
-            [
-                jnp.concatenate(
-                    [
-                        ref[pl.ds(lane * ROWS * SLOTS + j + q, SLOTS, stride=ROWS), :]
-                        for lane in range(NCOL // 128)
-                    ],
-                    axis=1,
-                )
-                for q in range(2)
-            ],
-            axis=0,
-        ).astype(jnp.bfloat16)
-
-    cosine = cos_ref[...]
-    sine = sin_ref[...]
     for j in range(0, ROWS, 2):
-        wave_re = wave(real_ref, j)
-        wave_im = wave(imag_ref, j)
-        across_re = product(cosine, wave_re) + product(sine, wave_im)
-        across_im = product(cosine, wave_im) - product(sine, wave_re)
-        for part, across in ((0, across_re), (1, across_im)):
+        waves = [[], []]
+        for q in range(2):
+            real, imag = parts(real_ref, j + q), parts(imag_ref, j + q)
+            for odd in range(2):
+                waves[odd].append(jnp.concatenate(real[odd] + imag[odd], axis=1))
+        even, odd = (
+            lax.dot_general(
+                table_ref[k],
+                jnp.concatenate(waves[k], axis=0).astype(jnp.bfloat16),
+                contract,
+                preferred_element_type=jnp.float32,
+            )
+            for k in range(2)
+        )
+        for half, across in ((0, even + odd), (1, even - odd)):
             for q in range(2):
-                for i in range(COLS):
-                    at = i * BLOCK + part * ROWS + j + q
-                    wide_ref[pl.ds(at, DEVICES, stride=2 * ROWS), :] = across[
-                        i * DEVICES : (i + 1) * DEVICES, q * SLOTS : (q + 1) * SLOTS
-                    ]
+                for part in range(2):
+                    for block in range(COLS * GROUPS):
+                        i, g = block // GROUPS, block % GROUPS
+                        device = g * PIX + half * (PIX // 2)
+                        at = i * BLOCK + device * 2 * ROWS + q * ROWS + part * (ROWS // 2) + j // 2
+                        row = part * (NCOL // 2) + block * (PIX // 2)
+                        wide_ref[pl.ds(at, PIX // 2, stride=2 * ROWS), :] = across[
+                            row : row + PIX // 2, q * SLOTS : (q + 1) * SLOTS
+                        ]
     stores = []
     for i in range(COLS):
         out_ref[i] = (
@@ -186,38 +207,66 @@
         copy.wait()
 
 
-def focal_kernel(group_ref, pieces_ref, table_ref, keep_ref, early_ref, late_ref, gram_ref):
-    group = group_ref[0]
-    real = jnp.zeros((STACK, STACK), jnp.float32)
-    cross = jnp.zeros((STACK, STACK), jnp.float32)
-    for i in range(COLS):
+def focal_column(pieces_ref, table_ref, i):
+    halves = []
+    for odd in range(2):
         wave = jnp.concatenate(
             [
-                pieces_ref[g * PIX : (g + 1) * PIX, i].reshape(2 * NROW, SLOTS)
+                pieces_ref[g * PIX : (g + 1) * PIX, i, odd].reshape(NROW, SLOTS)
                 for g in range(GROUPS)
             ],
             axis=1,
         )
-        focal = [
-            jnp.dot(
-                table_ref[part * NROW : (part + 1) * NROW, :],
-                wave,
-                preferred_element_type=jnp.float32,
-            ).astype(jnp.bfloat16)
-            for part in range(2)
-        ]
+        halves.append(jnp.dot(table_ref[odd], wave, preferred_element_type=jnp.float32))
+    low = (halves[0] + halves[1]).astype(jnp.bfloat16)
+    high = (halves[0] - halves[1]).astype(jnp.bfloat16)
+    return [
+        jnp.concatenate([half[part * HALF : (part + 1) * HALF] for half in (low, high)], axis=0)
+        for part in range(2)
+    ]
+
+
+def add_gram(focal, turned, real, cross):
+    real += jnp.dot(turned[0], focal[0], preferred_element_type=jnp.float32)
+    real += jnp.dot(turned[1], focal[1], preferred_element_type=jnp.float32)
+    cross += jnp.dot(turned[0], focal[1], preferred_element_type=jnp.float32)
+    return real, cross
+
+
+def split(group, turned):
+    low, high = turned[:, :HALF], turned[:, HALF:]
+    return jnp.where(group == 0, low, high), jnp.where(group == 0, high, low)
+
+
+def focal_kernel(group_ref, pieces_ref, table_ref, keep_ref, send_ref, real_ref, cross_ref):
+    focal = focal_column(pieces_ref, table_ref, 0)
+    turned = [focal[part].T for part in range(2)]
+    for part in range(2):
+        keep_ref[part], send_ref[part] = split(group_ref[0], turned[part])
+    zero = jnp.zeros((STACK, STACK), jnp.float32)
+    real_ref[...], cross_ref[...] = add_gram(focal, turned, zero, zero)
+
+
+def more_focal_kernel(
+    group_ref, pieces_ref, table_ref, real_ref, cross_ref, keep_ref, second_ref, third_hbm, gram_ref,
+    third_ref, third_sem,
+):
+    real, cross = real_ref[...], cross_ref[...]
+    for i in range(1, COLS):
+        focal = focal_column(pieces_ref, table_ref, i)
         turned = [focal[part].T for part in range(2)]
         for part in range(2):
-            low, high = turned[part][:, :HALF], turned[part][:, HALF:]
-            keep_ref[part, i] = jnp.where(group == 0, low, high)
-            sent = jnp.where(group == 0, high, low)
-            if i < EARLY:
-                early_ref[part, i] = sent
+            at = (i - 1) * 2 + part
+            kept, sent = split(group_ref[0], turned[part])
+            keep_ref[at] = kept
+            if at < THIRD:
+                third_ref[at] = sent
             else:
-                late_ref[part, i - EARLY] = sent
-        real += jnp.dot(turned[0], focal[0], preferred_element_type=jnp.float32)
-        real += jnp.dot(turned[1], focal[1], preferred_element_type=jnp.float32)
-        cross += jnp.dot(turned[0], focal[1], preferred_element_type=jnp.float32)
+                second_ref[at - THIRD] = sent
+        if i * 2 == THIRD:
+            late = pltpu.make_async_copy(third_ref, third_hbm, third_sem)
+            late.start()
+        real, cross = add_gram(focal, turned, real, cross)
     imag = cross - cross.T
     row = lax.broadcasted_iota(jnp.int32, (STACK, STACK), 0)
     column = lax.broadcasted_iota(jnp.int32, (STACK, STACK), 1)
@@ -225,6 +274,7 @@
     for q in range(4):
         top, left = (q // 2) * 128, (q % 2) * 128
         gram_ref[pl.ds(q, 128, stride=4), :] = packed[top : top + 128, left : left + 128]
+    late.wait()
 
 
 def total_kernel(parts_ref, out_ref):
@@ -283,21 +333,23 @@
 
 
 def modes_kernel(
-    group_ref, left_ref, scale_ref, keep_ref, early_ref, late_ref, out_hbm,
-    wide_ref, out_ref, out_sem,
+    group_ref, left_ref, scale_ref, kept_ref, kept_more_ref, first_ref, second_ref, third_ref,
+    out_hbm,    wide_ref, out_ref, out_sem,
 ):
     group = group_ref[0]
     left = left_ref[...]
     scale = scale_ref[...]
+    sources = (
+        [kept_ref[part] for part in range(2)] + [kept_more_ref[at] for at in range(2 * COLS - 2)],
+        [first_ref[part] for part in range(2)]
+        + [third_ref[at] for at in range(THIRD)]
+        + [second_ref[at] for at in range(2 * COLS - 2 - THIRD)],
+    )
     for source in range(2):
         first = jnp.where(group == source, 0, COLS)
         for i in range(COLS):
-            ref, at = keep_ref, i
-            if source == 1:
-                ref, at = (early_ref, i) if i < EARLY else (late_ref, i - EARLY)
-            mode = jnp.dot(
-                left, ref[:, at].reshape(2 * STACK, HALF), preferred_element_type=jnp.float32
-            )
+            focal = jnp.concatenate(sources[source][2 * i : 2 * i + 2], axis=0)
+            mode = jnp.dot(left, focal, preferred_element_type=jnp.float32)
             for part in range(2):
                 for lane in range(HALF // 128):
                     rows = pl.ds(
@@ -330,11 +382,11 @@
 
 def local(fields, lens_phase, occupancy, focus_scale, assignment, start_basis):
     group = lax.axis_index("grp").astype(jnp.int32).reshape(1)
-    cos_cols, sin_cols = (jnp.asarray(table) for table in column_tables())
+    column_table = jnp.asarray(column_tables())
     across = pl.pallas_call(
         spectra_kernel,
         out_shape=jax.ShapeDtypeStruct((DEVICES, COLS, 2 * ROWS, SLOTS), jnp.bfloat16),
-        in_specs=[SMEM] + [HBM] * 7,
+        in_specs=[SMEM] + [HBM] * 6,
         out_specs=HBM,
         scratch_shapes=[
             pltpu.SMEM((STACK,), jnp.int32),
@@ -342,8 +394,7 @@
             pltpu.SMEM((STACK,), jnp.float32),
             pltpu.VMEM((2, SLOTS, ROWS, NCOL), jnp.bfloat16),
             pltpu.VMEM((ROWS, NCOL), jnp.float32),
-            pltpu.VMEM((NCOL, NCOL), jnp.bfloat16),
-            pltpu.VMEM((NCOL, NCOL), jnp.bfloat16),
+            pltpu.VMEM((2, NCOL, NCOL), jnp.bfloat16),
             pltpu.VMEM((NCOL // 128 * ROWS * SLOTS, 128), jnp.float32),
             pltpu.VMEM((NCOL // 128 * ROWS * SLOTS, 128), jnp.float32),
             pltpu.VMEM((COLS * BLOCK, SLOTS), jnp.float32),
@@ -355,27 +406,41 @@
         ],
         compiler_params=params(54),
         name="spectra",
-    )(group, assignment, occupancy, focus_scale, fields[0], lens_phase, cos_cols, sin_cols)
+    )(group, assignment, occupancy, focus_scale, fields[0], lens_phase, column_table)
     pieces = lax.all_to_all(across, AXES, 0, 0, tiled=True)
+    pieces = pieces.reshape(DEVICES, COLS, 2, ROWS, SLOTS)
+
 
     def focal_shape(count):
-        return jax.ShapeDtypeStruct((2, count, STACK, HALF), jnp.bfloat16)
-
-    keep, early, late, gram = pl.pallas_call(
+        return jax.ShapeDtypeStruct((count, STACK, HALF), jnp.bfloat16)
+
+    row_table = jnp.asarray(row_tables())
+    square = jax.ShapeDtypeStruct((STACK, STACK), jnp.float32)
+    kept, swap_first, real, cross = pl.pallas_call(
         focal_kernel,
+        out_shape=(focal_shape(2), focal_shape(2), square, square),
+        in_specs=[SMEM] + [VMEM] * 2,
+        out_specs=(VMEM,) * 4,
+        compiler_params=params(12),
+        name="focal",
+    )(group, pieces, row_table)
+    kept_more, swap_second, swap_third, gram = pl.pallas_call(
+        more_focal_kernel,
         out_shape=(
-            focal_shape(COLS),
-            focal_shape(EARLY),
-            focal_shape(COLS - EARLY),
+            focal_shape(2 * COLS - 2),
+            focal_shape(2 * COLS - 2 - THIRD),
+            pltpu.HBM((THIRD, STACK, HALF), jnp.bfloat16),
             jax.ShapeDtypeStruct((4 * DEVICES, 128), jnp.float32),
         ),
-        in_specs=[SMEM] + [VMEM] * 2,
-        out_specs=(VMEM,) * 4,
-        compiler_params=params(20),
-        name="focal",
-    )(group, pieces, jnp.asarray(row_tables()))
-    early = lax.ppermute(early, "grp", [(0, 1), (1, 0)])
-    late = lax.ppermute(late, "grp", [(0, 1), (1, 0)])
+        in_specs=[SMEM] + [VMEM] * 4,
+        out_specs=(VMEM, VMEM, HBM, VMEM),
+        scratch_shapes=[pltpu.VMEM((THIRD, STACK, HALF), jnp.bfloat16), pltpu.SemaphoreType.DMA],
+        compiler_params=params(12),
+        name="more_focal",
+    )(group, pieces, row_table, real, cross)
+    swap_first = lax.ppermute(swap_first, "grp", [(0, 1), (1, 0)])
+    swap_second = lax.ppermute(swap_second, "grp", [(0, 1), (1, 0)])
+    swap_third = lax.ppermute(swap_third, "grp", [(0, 1), (1, 0)])
     parts = lax.all_to_all(gram.reshape(DEVICES, 4, 128), AXES, 0, 0, tiled=True)
     total = pl.pallas_call(
         total_kernel,
@@ -401,7 +466,7 @@
     coherent_modes = pl.pallas_call(
         modes_kernel,
         out_shape=jax.ShapeDtypeStruct((2, RANK, GROUPS * COLS, HALF), jnp.bfloat16),
-        in_specs=[SMEM] + [VMEM] * 5,
+        in_specs=[SMEM] + [VMEM] * 7,
         out_specs=HBM,
         scratch_shapes=[
             pltpu.VMEM((2 * HALF // 128 * WIDE, 128), jnp.float32),
@@ -410,7 +475,7 @@
         ],
         compiler_params=params(16),
         name="modes",
-    )(group, left, scale, keep, early, late)
+    )(group, left, scale, kept, kept_more, swap_first, swap_second, swap_third)
     return coherent_modes, power.reshape(RANK)
 
 

time: 105 us -> 94.9 us (0.904)
  blocking collectives: 83.1 us -> 56.1 us
  waiting for transfers between devices: 0.01 us -> 9.08 us
  starting transfers between devices: 3.05 us -> 10.7 us
    all_to_all x1 -> x0, blocking collectives: 26.6 us -> none  [local(): lax.all_to_all(gram.reshape(DEVICES, 4, 128), AXES, 0, 0, tiled=True)]
    all_to_all x0 -> x1, waiting for transfers between devices: none -> 9.07 us  [local(): lax.all_to_all(gram.reshape(DEVICES, 4, 128), AXES, 0, 0, tiled=True)]
    all_to_all x0 -> x1, starting transfers between devices: none -> 6.11 us  [local(): lax.all_to_all(gram.reshape(DEVICES, 4, 128), AXES, 0, 0, tiled=True)]
    ppermute x2 -> x3, starting transfers between devices: 3.05 us -> 4.63 us  [the longest x1 3.33 us: local(): swap_third = lax.ppermute(swap_third, 'grp', [(0, 1), (1, 0)])]
    pallas_call x1 -> x2, Pallas kernels: 3.94 us -> 3.99 us  [the longest x1 3.04 us: local(): pl.pallas_call(more_focal_kernel, out_shape=(focal_shape(2 * COLS - 2), f...]
  transfers between devices with their start and end apart: 2 -> 4, of which waited for: 0 -> 1; matrix products, arithmetic and copies ran while one was open for 0% -> 0% of each run, Pallas kernels for 3% -> 3%
where the time goes in v1:
time: 94.9 us; the launch traced here: 94.6 us
  blocking collectives  56.1 us (59%)
  Pallas kernels  18 us (19%)
  starting transfers between devices  10.7 us (11%)
  waiting for transfers between devices  9.08 us (10%)
    all_to_all x1, blocking collectives, local(): pieces = lax.all_to_all(across, AXES, 0, 0, tiled=True)  41.6 us
    all_to_all x1, blocking collectives, local(): lax.all_to_all(total.reshape(DEVICES, 4, 128), AXES, 0, 0, tiled=True)  14.5 us
    all_to_all x1, waiting for transfers between devices, local(): lax.all_to_all(gram.reshape(DEVICES, 4, 128), AXES, 0, 0, tiled=True)  9.07 us
    pallas_call x1, Pallas kernels, local(): pl.pallas_call(spectra_kernel, out_shape=jax.ShapeDtypeStruct((DEVICES, C...  8.8 us
    all_to_all x1, starting transfers between devices, local(): lax.all_to_all(gram.reshape(DEVICES, 4, 128), AXES, 0, 0, tiled=True)  6.11 us
    ppermute x1, starting transfers between devices, local(): swap_third = lax.ppermute(swap_third, 'grp', [(0, 1), (1, 0)])  3.33 us
    pallas_call x1, Pallas kernels, local(): pl.pallas_call(power_kernel, out_shape=(jax.ShapeDtypeStruct((2 * RANK, 2...  3.16 us
    pallas_call x1, Pallas kernels, local(): pl.pallas_call(more_focal_kernel, out_shape=(focal_shape(2 * COLS - 2), f...  3.04 us
  transfers between devices with their start and end apart: 4, of which 1 were waited for; matrix products, arithmetic and copies ran while one was open for 0% of the time, Pallas kernels for 3%

profile of v1, /device:TPU:1, one launch (start us, length us, event | category | flops | bytes accessed | tf_op | source)
XLA Modules:
  0.0 94.6 jit_solution(465777172411091059)
XLA Ops:
  0.6 8.8 %spectra.1 = bf16[128,4,16,128]{3,2,1,0:T(8,128)(2,1)} custom-call(s32[1]{0:T(128)} %bitcast.group_ref, s32[256]{0:T(256)} %assign_hbm.1, f32[256]{0:T(256)} %occ_hbm.1, f32[256]{0:T(256)} %chrom_hbm.1, bf16[2,128,8,512]{3,2,1,0:T(8,128)(2,1)} %bitcast.13, f32[8,512]{1,0:T(8,128)} %lens_hbm.1, bf16[2,512,512]{2,1,0:T(8,128)(2,1)} %constant.10.clone.table_hbm), custom_call_target="tpu_custom_call" | custom-call | tf_op jit(solution)/shard_map/spectra/pallas_call | solution.py:386
  9.4 0.0 copy-start
  9.5 41.6 %all_to_all.15 = bf16[128,4,16,128]{3,2,1,0:T(8,128)(2,1)S(1)} all-to-all(bf16[128,4,16,128]{3,2,1,0:T(8,128)(2,1)} %spectra.1), channel_id=1, replica_groups=mesh['grp'=2,'pix'=64] {'grp','pix'}, dimensions={0} | all-to-all | bytes 4194304 | tf_op jit(solution)/shard_map/all_to_all | solution.py:410
  51.1 0.0 copy-done
  51.1 0.9 %focal.1 = (bf16[2,256,256]{2,1,0:T(8,128)(2,1)S(1)}, bf16[2,256,256]{2,1,0:T(8,128)(2,1)S(1)}, f32[256,256]{1,0:T(8,128)S(1)}, f32[256,256]{1,0:T(8,128)S(1)}) custom-call(s32[1]{0:T(128)} %bitcast.group_ref, bf16[128,4,2,8,128]{4,3,2,1,0:T(8,128)(2,1)S(1)} %bitcast.8, bf16[2,512,512]{2,1,0:T(8,128)(2,1)S(1)} %copy-done), custom_call_target="tpu_custom_call" | custom-call | tf_op jit(solution)/shard_map/focal/pallas_call | solution.py:419
  52.0 0.0 copy-start.1
  52.0 3.0 %more_focal.1 = (bf16[6,256,256]{2,1,0:T(8,128)(2,1)S(1)}, bf16[4,256,256]{2,1,0:T(8,128)(2,1)S(1)}, bf16[2,256,256]{2,1,0:T(8,128)(2,1)}, f32[512,128]{1,0:T(8,128)}) custom-call(s32[1]{0:T(128)} %bitcast.group_ref, bf16[128,4,2,8,128]{4,3,2,1,0:T(8,128)(2,1)S(1)} %bitcast.9, bf16[2,512,512]{2,1,0:T(8,128)(2,1)S(1)} %copy-done, ...), custom_call_target="tpu_custom_call" | custom-call | tf_op jit(solution)/shard_map/more_focal/pallas_call | solution.py:427
  55.1 1.2 %collective-permute-start.1 = (bf16[4,256,256]{2,1,0:T(8,128)(2,1)S(1)}, bf16[4,256,256]{2,1,0:T(8,128)(2,1)S(1)}, u32[]{:S(2)}, u32[]{:S(2)}) collective-permute-start(bf16[4,256,256]{2,1,0:T(8,128)(2,1)S(1)} %get-tuple-element.21), channel_id=1, source_target_pairs={{0,64},{64,0},{1,65},{65,1},{2,66},{66,2},{3,67},{67,3},{4,68},{68... | collective-permute-start | bytes 1572872 | tf_op jit(solution)/shard_map/ppermute | solution.py:442
  56.3 6.1 %all-to-all-start.1 = ((f32[128,4,128]{2,1,0:T(4,128)}), f32[128,4,128]{2,1,0:T(4,128)S(1)}, u32[]{:S(2)}, u32[]{:S(2)}) async-start(f32[128,4,128]{2,1,0:T(4,128)} %bitcast.3), calls=%async_computation.1 | async-start | bytes 524288 | tf_op jit(solution)/shard_map/all_to_all | solution.py:444
  62.4 3.3 %collective-permute-start.2 = (bf16[2,256,256]{2,1,0:T(8,128)(2,1)}, bf16[2,256,256]{2,1,0:T(8,128)(2,1)S(1)}, u32[]{:S(2)}, u32[]{:S(2)}) collective-permute-start(bf16[2,256,256]{2,1,0:T(8,128)(2,1)} %get-tuple-element.22), channel_id=1, source_target_pairs={{0,64},{64,0},{1,65},{65,1},{2,66},{66,2},{3,67},{67,3},{4,68},{68... | collective-permute-start | bytes 786440 | tf_op jit(solution)/shard_map/ppermute | solution.py:443
  65.7 0.1 collective-permute-start
  65.8 9.1 %all-to-all-done.1 = f32[128,4,128]{2,1,0:T(4,128)S(1)} async-done(((f32[128,4,128]{2,1,0:T(4,128)}), f32[128,4,128]{2,1,0:T(4,128)S(1)}, u32[]{:S(2)}, u32[]{:S(2)}) %all-to-all-start.1) | async-done | bytes 262176 | tf_op jit(solution)/shard_map/all_to_all | solution.py:444
  74.9 0.1 total.1
  75.0 14.5 %all_to_all.16 = f32[128,4,128]{2,1,0:T(4,128)S(1)} all-to-all(f32[128,4,128]{2,1,0:T(4,128)S(1)} %bitcast.12), channel_id=1, replica_groups=mesh['grp'=2,'pix'=64] {'grp','pix'}, dimensions={0} | all-to-all | bytes 524288 | tf_op jit(solution)/shard_map/all_to_all | solution.py:453
  89.5 0.0 copy-done.1
  89.5 3.2 %power.1 = (bf16[256,512]{1,0:T(8,128)(2,1)S(1)}, f32[128,128]{1,0:T(8,128)S(1)}, f32[1,128]{1,0:T(1,128)}) custom-call(f32[512,128]{1,0:T(8,128)S(1)} %bitcast.11, f32[2,256,128]{2,1,0:T(8,128)S(1)} %copy-done.1), custom_call_target="tpu_custom_call" | custom-call | tf_op jit(solution)/shard_map/power/pallas_call | solution.py:454
  92.7 0.0 collective-permute-done.2.third_ref
  92.7 0.0 collective-permute-done.first_ref
  92.7 0.0 collective-permute-done.1.second_ref
  92.7 1.9 %modes.1 = bf16[2,128,8,256]{3,2,1,0:T(8,128)(2,1)} custom-call(s32[1]{0:T(128)} %bitcast.group_ref, bf16[256,512]{1,0:T(8,128)(2,1)S(1)} %get-tuple-element.16.left_ref, f32[128,128]{1,0:T(8,128)S(1)} %get-tuple-element.17.scale_ref, bf16[2,256,256]{2,1,0:T(8,128)(2,1)S(1)} %get-tuple-element.18.kept_ref, ...), custom_call_target="tpu_custom_call" | custom-call | tf_op jit(solution)/shard_map/modes/pallas_call | solution.py:466
Async XLA Ops:
  9.4 41.6 %copy-start = (bf16[2,512,512]{2,1,0:T(8,128)(2,1)S(1)}, bf16[2,512,512]{2,1,0:T(8,128)(2,1)}, u32[]{:S(2)}) copy-start(bf16[2,512,512]{2,1,0:T(8,128)(2,1)} %constant.11.clone.table_ref) | copy-start | bytes 3145732
  52.0 37.5 %copy-start.1 = (f32[2,256,128]{2,1,0:T(8,128)S(1)}, f32[2,256,128]{2,1,0:T(8,128)}, u32[]{:S(2)}) copy-start(f32[2,256,128]{2,1,0:T(8,128)} %start_ref.1) | copy-start | bytes 786436
  55.1 37.6 %collective-permute-start.1 = (bf16[4,256,256]{2,1,0:T(8,128)(2,1)S(1)}, bf16[4,256,256]{2,1,0:T(8,128)(2,1)S(1)}, u32[]{:S(2)}, u32[]{:S(2)}) collective-permute-start(bf16[4,256,256]{2,1,0:T(8,128)(2,1)S(1)} %get-tuple-element.21), channel_id=1, source_target_pairs={{0,64},{64,0},{1,65},{65,1},{2,66},{66,2},{3,67},{67,3},{4,68},{68... | collective-permute-start | bytes 1572872 | tf_op jit(solution)/shard_map/ppermute | solution.py:442
  56.3 18.6 %all-to-all-start.1 = ((f32[128,4,128]{2,1,0:T(4,128)}), f32[128,4,128]{2,1,0:T(4,128)S(1)}, u32[]{:S(2)}, u32[]{:S(2)}) async-start(f32[128,4,128]{2,1,0:T(4,128)} %bitcast.3), calls=%async_computation.1 | async-start | bytes 524288 | tf_op jit(solution)/shard_map/all_to_all | solution.py:444
  62.4 30.3 %collective-permute-start.2 = (bf16[2,256,256]{2,1,0:T(8,128)(2,1)}, bf16[2,256,256]{2,1,0:T(8,128)(2,1)S(1)}, u32[]{:S(2)}, u32[]{:S(2)}) collective-permute-start(bf16[2,256,256]{2,1,0:T(8,128)(2,1)} %get-tuple-element.22), channel_id=1, source_target_pairs={{0,64},{64,0},{1,65},{65,1},{2,66},{66,2},{3,67},{67,3},{4,68},{68... | collective-permute-start | bytes 786440 | tf_op jit(solution)/shard_map/ppermute | solution.py:443
  65.7 26.9 %collective-permute-start = (bf16[2,256,256]{2,1,0:T(8,128)(2,1)S(1)}, bf16[2,256,256]{2,1,0:T(8,128)(2,1)S(1)}, u32[]{:S(2)}, u32[]{:S(2)}) collective-permute-start(bf16[2,256,256]{2,1,0:T(8,128)(2,1)S(1)} %get-tuple-element.20), channel_id=1, source_target_pairs={{0,64},{64,0},{1,65},{65,1},{2,66},{66,2},{3,67},{67,3},{4,68},{68... | collective-permute-start | bytes 786440 | tf_op jit(solution)/shard_map/ppermute | solution.py:441

commit v2 on v1

--- a/solution.py
+++ b/solution.py
@@ -24,7 +24,7 @@
 THIRD = 2
 CHUNKS = 4
 CHUNK = SLOTS // CHUNKS
-BLOCK = DEVICES * 2 * ROWS
+PLANE = DEVICES * COLS + 1
 AXES = ("grp", "pix")
 
 LIMIT = 0.5 * 1.5 * 3.140625
@@ -89,9 +89,9 @@
 
 
 def spectra_kernel(
-    group_ref, assign_hbm, occ_hbm, chrom_hbm, fields_hbm, lens_hbm, table_hbm, out_hbm,
+    group_ref, assign_hbm, occ_hbm, chrom_hbm, fields_hbm, lens_hbm, table_hbm, out_ref,
     assign_ref, occ_ref, chrom_ref, fields_ref, lens_ref, table_ref,
-    real_ref, imag_ref, wide_ref, out_ref, small_sem, field_sem, table_sem, out_sem,
+    real_ref, imag_ref, wide_ref, small_sem, field_sem, table_sem,
 ):
     def chunk(part, c):
         slots = pl.ds(c * CHUNK, CHUNK)
@@ -148,7 +148,7 @@
     for c in range(CHUNKS):
         for part in range(2):
             chunk(part, c).wait()
-        lax.fori_loop(c * CHUNK, (c + 1) * CHUNK, phase, 0, unroll=4)
+        lax.fori_loop(c * CHUNK, (c + 1) * CHUNK, phase, 0, unroll=16)
     for copy in large:
         copy.wait()
     lane = lax.broadcasted_iota(jnp.int32, (SLOTS, 128), 1)
@@ -189,22 +189,19 @@
                     for block in range(COLS * GROUPS):
                         i, g = block // GROUPS, block % GROUPS
                         device = g * PIX + half * (PIX // 2)
-                        at = i * BLOCK + device * 2 * ROWS + q * ROWS + part * (ROWS // 2) + j // 2
+                        at = q * ROWS + part * (ROWS // 2) + j // 2
                         row = part * (NCOL // 2) + block * (PIX // 2)
-                        wide_ref[pl.ds(at, PIX // 2, stride=2 * ROWS), :] = across[
+                        wide_ref[pl.ds(at * PLANE + i * DEVICES + device, PIX // 2), :] = across[
                             row : row + PIX // 2, q * SLOTS : (q + 1) * SLOTS
                         ]
-    stores = []
     for i in range(COLS):
-        out_ref[i] = (
-            wide_ref[i * BLOCK : (i + 1) * BLOCK, :]
-            .astype(jnp.bfloat16)
-            .reshape(DEVICES, 2 * ROWS, SLOTS)
-        )
-        stores.append(pltpu.make_async_copy(out_ref.at[i], out_hbm.at[:, i], out_sem.at[i]))
-        stores[-1].start()
-    for copy in stores:
-        copy.wait()
+
+        def gather(d, carry):
+            rows = wide_ref[pl.ds(i * DEVICES + d, 2 * ROWS, stride=PLANE), :]
+            out_ref[d, i] = rows.astype(jnp.bfloat16)
+            return carry
+
+        lax.fori_loop(0, DEVICES, gather, 0, unroll=8)
 
 
 def focal_column(pieces_ref, table_ref, i):
@@ -296,13 +293,23 @@
     gram_im = jnp.where(row > column, packed, jnp.where(row == column, 0.0, -turned))
     gram = jnp.concatenate([gram_re, gram_im], axis=0)
 
+    def pieces(value):
+        first = value.astype(jnp.bfloat16)
+        rest = value - first.astype(jnp.float32)
+        second = rest.astype(jnp.bfloat16)
+        return first, second, (rest - second.astype(jnp.float32)).astype(jnp.bfloat16)
+
+    grams = pieces(gram)
+    left = jnp.concatenate([grams[k] for k in (0, 1, 2, 0, 1, 0)], axis=1)
+
     def apply(re, im):
-        both = jnp.dot(
-            gram,
-            jnp.concatenate([re, im], axis=1),
-            precision=lax.Precision.HIGHEST,
-            preferred_element_type=jnp.float32,
-        )
+        both = jnp.concatenate([re, im], axis=1)
+        if both.dtype == jnp.bfloat16:
+            right = jnp.concatenate([both] * 3, axis=0)
+        else:
+            right = pieces(both)
+            right = jnp.concatenate([right[k] for k in (0, 0, 0, 1, 1, 2)], axis=0)
+        both = jnp.dot(left[:, : right.shape[0]], right, preferred_element_type=jnp.float32)
         return (
             both[:STACK, :RANK] - both[STACK:, RANK:],
             both[:STACK, RANK:] + both[STACK:, :RANK],
@@ -316,9 +323,11 @@
         )
         basis_re = image_re / norm
         basis_im = image_im / norm
-    rounded_re = basis_re.astype(jnp.bfloat16).astype(jnp.float32)
-    rounded_im = basis_im.astype(jnp.bfloat16).astype(jnp.float32)
+    rounded_re = basis_re.astype(jnp.bfloat16)
+    rounded_im = basis_im.astype(jnp.bfloat16)
     image_re, image_im = apply(rounded_re, rounded_im)
+    rounded_re = rounded_re.astype(jnp.float32)
+    rounded_im = rounded_im.astype(jnp.float32)
     energy = jnp.sum(rounded_re * image_re + rounded_im * image_im, axis=0, keepdims=True)
     trace = jnp.sum(jnp.where(row == column, packed, 0.0))
     power_ref[...] = energy * STACK / trace
@@ -387,7 +396,7 @@
         spectra_kernel,
         out_shape=jax.ShapeDtypeStruct((DEVICES, COLS, 2 * ROWS, SLOTS), jnp.bfloat16),
         in_specs=[SMEM] + [HBM] * 6,
-        out_specs=HBM,
+        out_specs=VMEM,
         scratch_shapes=[
             pltpu.SMEM((STACK,), jnp.int32),
             pltpu.SMEM((STACK,), jnp.float32),
@@ -397,16 +406,22 @@
             pltpu.VMEM((2, NCOL, NCOL), jnp.bfloat16),
             pltpu.VMEM((NCOL // 128 * ROWS * SLOTS, 128), jnp.float32),
             pltpu.VMEM((NCOL // 128 * ROWS * SLOTS, 128), jnp.float32),
-            pltpu.VMEM((COLS * BLOCK, SLOTS), jnp.float32),
-            pltpu.VMEM((COLS, DEVICES, 2 * ROWS, SLOTS), jnp.bfloat16),
+            pltpu.VMEM((2 * ROWS * PLANE, SLOTS), jnp.float32),
             pltpu.SemaphoreType.DMA((4,)),
             pltpu.SemaphoreType.DMA((2, CHUNKS)),
             pltpu.SemaphoreType.DMA((2,)),
-            pltpu.SemaphoreType.DMA((COLS,)),
         ],
-        compiler_params=params(54),
+        compiler_params=params(24),
         name="spectra",
-    )(group, assignment, occupancy, focus_scale, fields[0], lens_phase, column_table)
+    )(
+        group,
+        *(
+            pltpu.with_memory_space_constraint(array, pltpu.HBM)
+            for array in (
+                assignment, occupancy, focus_scale, fields[0], lens_phase, column_table
+            )
+        ),
+    )
     pieces = lax.all_to_all(across, AXES, 0, 0, tiled=True)
     pieces = pieces.reshape(DEVICES, COLS, 2, ROWS, SLOTS)
 

time: 94.9 us -> 92.1 us (0.970)
  Pallas kernels: 18 us -> 15.5 us
    pallas_call x1, Pallas kernels: 8.8 us -> 6.52 us  [local(): pl.pallas_call(spectra_kernel, out_shape=jax.ShapeDtypeStruct((DEVICES, C...]
where the time goes in v2:
time: 92.1 us; the launch traced here: 91.9 us
  blocking collectives  55.9 us (61%)
  Pallas kernels  15.5 us (17%)
  starting transfers between devices  10.8 us (12%)
  waiting for transfers between devices  9.07 us (10%)
    all_to_all x1, blocking collectives, local(): pieces = lax.all_to_all(across, AXES, 0, 0, tiled=True)  41.4 us
    all_to_all x1, blocking collectives, local(): lax.all_to_all(total.reshape(DEVICES, 4, 128), AXES, 0, 0, tiled=True)  14.5 us
    all_to_all x1, waiting for transfers between devices, local(): lax.all_to_all(gram.reshape(DEVICES, 4, 128), AXES, 0, 0, tiled=True)  9.07 us
    pallas_call x1, Pallas kernels, local(): pl.pallas_call(spectra_kernel, out_shape=jax.ShapeDtypeStruct((DEVICES, C...  6.52 us
    all_to_all x1, starting transfers between devices, local(): lax.all_to_all(gram.reshape(DEVICES, 4, 128), AXES, 0, 0, tiled=True)  6.12 us
    ppermute x1, starting transfers between devices, local(): swap_third = lax.ppermute(swap_third, 'grp', [(0, 1), (1, 0)])  3.33 us
    pallas_call x1, Pallas kernels, local(): pl.pallas_call(more_focal_kernel, out_shape=(focal_shape(2 * COLS - 2), f...  3.06 us
    pallas_call x1, Pallas kernels, local(): pl.pallas_call(power_kernel, out_shape=(jax.ShapeDtypeStruct((2 * RANK, 2...  2.94 us
  transfers between devices with their start and end apart: 4, of which 1 were waited for; matrix products, arithmetic and copies ran while one was open for 0% of the time, Pallas kernels for 3%

profile of v2, /device:TPU:1, one launch (start us, length us, event | category | flops | bytes accessed | tf_op | source)
XLA Modules:
  0.0 91.9 jit_solution(3047993457263064694)
XLA Ops:
  0.6 6.5 %spectra.1 = bf16[128,4,16,128]{3,2,1,0:T(8,128)(2,1)S(1)} custom-call(s32[1]{0:T(128)} %bitcast.group_ref, s32[256]{0:T(256)} %assign_hbm.1, f32[256]{0:T(256)} %occ_hbm.1, f32[256]{0:T(256)} %chrom_hbm.1, bf16[2,128,8,512]{3,2,1,0:T(8,128)(2,1)} %bitcast.13, f32[8,512]{1,0:T(8,128)} %lens_hbm.1, bf16[2,512,512]{2,1,0:T(8,128)(2,1)} %constant.10.clone.table_hbm), custom_call_target="tpu_custom_call" | custom-call | tf_op jit(solution)/shard_map/spectra/pallas_call | solution.py:395
  7.2 0.0 copy-start
  7.2 41.4 %all_to_all.15 = bf16[128,4,16,128]{3,2,1,0:T(8,128)(2,1)S(1)} all-to-all(bf16[128,4,16,128]{3,2,1,0:T(8,128)(2,1)S(1)} %spectra.1), channel_id=1, replica_groups=mesh['grp'=2,'pix'=64] {'grp','pix'}, dimensions={0} | all-to-all | bytes 4194304 | tf_op jit(solution)/shard_map/all_to_all | solution.py:425
  48.6 0.0 copy-done
  48.6 0.9 %focal.1 = (bf16[2,256,256]{2,1,0:T(8,128)(2,1)S(1)}, bf16[2,256,256]{2,1,0:T(8,128)(2,1)S(1)}, f32[256,256]{1,0:T(8,128)S(1)}, f32[256,256]{1,0:T(8,128)S(1)}) custom-call(s32[1]{0:T(128)} %bitcast.group_ref, bf16[128,4,2,8,128]{4,3,2,1,0:T(8,128)(2,1)S(1)} %bitcast.8, bf16[2,512,512]{2,1,0:T(8,128)(2,1)S(1)} %copy-done), custom_call_target="tpu_custom_call" | custom-call | tf_op jit(solution)/shard_map/focal/pallas_call | solution.py:434
  49.5 0.0 copy-start.1
  49.5 3.1 %more_focal.1 = (bf16[6,256,256]{2,1,0:T(8,128)(2,1)S(1)}, bf16[4,256,256]{2,1,0:T(8,128)(2,1)S(1)}, bf16[2,256,256]{2,1,0:T(8,128)(2,1)}, f32[512,128]{1,0:T(8,128)}) custom-call(s32[1]{0:T(128)} %bitcast.group_ref, bf16[128,4,2,8,128]{4,3,2,1,0:T(8,128)(2,1)S(1)} %bitcast.9, bf16[2,512,512]{2,1,0:T(8,128)(2,1)S(1)} %copy-done, ...), custom_call_target="tpu_custom_call" | custom-call | tf_op jit(solution)/shard_map/more_focal/pallas_call | solution.py:442
  52.6 1.2 %collective-permute-start.1 = (bf16[4,256,256]{2,1,0:T(8,128)(2,1)S(1)}, bf16[4,256,256]{2,1,0:T(8,128)(2,1)S(1)}, u32[]{:S(2)}, u32[]{:S(2)}) collective-permute-start(bf16[4,256,256]{2,1,0:T(8,128)(2,1)S(1)} %get-tuple-element.21), channel_id=1, source_target_pairs={{0,64},{64,0},{1,65},{65,1},{2,66},{66,2},{3,67},{67,3},{4,68},{68... | collective-permute-start | bytes 1572872 | tf_op jit(solution)/shard_map/ppermute | solution.py:457
  53.8 6.1 %all-to-all-start.1 = ((f32[128,4,128]{2,1,0:T(4,128)}), f32[128,4,128]{2,1,0:T(4,128)S(1)}, u32[]{:S(2)}, u32[]{:S(2)}) async-start(f32[128,4,128]{2,1,0:T(4,128)} %bitcast.3), calls=%async_computation.1 | async-start | bytes 524288 | tf_op jit(solution)/shard_map/all_to_all | solution.py:459
  59.9 3.3 %collective-permute-start.2 = (bf16[2,256,256]{2,1,0:T(8,128)(2,1)}, bf16[2,256,256]{2,1,0:T(8,128)(2,1)S(1)}, u32[]{:S(2)}, u32[]{:S(2)}) collective-permute-start(bf16[2,256,256]{2,1,0:T(8,128)(2,1)} %get-tuple-element.22), channel_id=1, source_target_pairs={{0,64},{64,0},{1,65},{65,1},{2,66},{66,2},{3,67},{67,3},{4,68},{68... | collective-permute-start | bytes 786440 | tf_op jit(solution)/shard_map/ppermute | solution.py:458
  63.3 0.1 collective-permute-start
  63.4 9.1 %all-to-all-done.1 = f32[128,4,128]{2,1,0:T(4,128)S(1)} async-done(((f32[128,4,128]{2,1,0:T(4,128)}), f32[128,4,128]{2,1,0:T(4,128)S(1)}, u32[]{:S(2)}, u32[]{:S(2)}) %all-to-all-start.1) | async-done | bytes 262176 | tf_op jit(solution)/shard_map/all_to_all | solution.py:459
  72.4 0.1 total.1
  72.5 14.5 %all_to_all.16 = f32[128,4,128]{2,1,0:T(4,128)S(1)} all-to-all(f32[128,4,128]{2,1,0:T(4,128)S(1)} %bitcast.12), channel_id=1, replica_groups=mesh['grp'=2,'pix'=64] {'grp','pix'}, dimensions={0} | all-to-all | bytes 524288 | tf_op jit(solution)/shard_map/all_to_all | solution.py:468
  87.0 0.0 copy-done.1
  87.0 2.9 %power.1 = (bf16[256,512]{1,0:T(8,128)(2,1)S(1)}, f32[128,128]{1,0:T(8,128)S(1)}, f32[1,128]{1,0:T(1,128)}) custom-call(f32[512,128]{1,0:T(8,128)S(1)} %bitcast.11, f32[2,256,128]{2,1,0:T(8,128)S(1)} %copy-done.1), custom_call_target="tpu_custom_call" | custom-call | tf_op jit(solution)/shard_map/power/pallas_call | solution.py:469
  90.0 0.0 collective-permute-done.2.third_ref
  90.0 0.0 collective-permute-done.first_ref
  90.0 0.0 collective-permute-done.1.second_ref
  90.0 1.9 %modes.1 = bf16[2,128,8,256]{3,2,1,0:T(8,128)(2,1)} custom-call(s32[1]{0:T(128)} %bitcast.group_ref, bf16[256,512]{1,0:T(8,128)(2,1)S(1)} %get-tuple-element.16.left_ref, f32[128,128]{1,0:T(8,128)S(1)} %get-tuple-element.17.scale_ref, bf16[2,256,256]{2,1,0:T(8,128)(2,1)S(1)} %get-tuple-element.18.kept_ref, ...), custom_call_target="tpu_custom_call" | custom-call | tf_op jit(solution)/shard_map/modes/pallas_call | solution.py:481
Async XLA Ops:
  7.2 41.4 %copy-start = (bf16[2,512,512]{2,1,0:T(8,128)(2,1)S(1)}, bf16[2,512,512]{2,1,0:T(8,128)(2,1)}, u32[]{:S(2)}) copy-start(bf16[2,512,512]{2,1,0:T(8,128)(2,1)} %constant.11.clone.table_ref) | copy-start | bytes 3145732
  49.5 37.5 %copy-start.1 = (f32[2,256,128]{2,1,0:T(8,128)S(1)}, f32[2,256,128]{2,1,0:T(8,128)}, u32[]{:S(2)}) copy-start(f32[2,256,128]{2,1,0:T(8,128)} %start_ref.1) | copy-start | bytes 786436
  52.6 37.4 %collective-permute-start.1 = (bf16[4,256,256]{2,1,0:T(8,128)(2,1)S(1)}, bf16[4,256,256]{2,1,0:T(8,128)(2,1)S(1)}, u32[]{:S(2)}, u32[]{:S(2)}) collective-permute-start(bf16[4,256,256]{2,1,0:T(8,128)(2,1)S(1)} %get-tuple-element.21), channel_id=1, source_target_pairs={{0,64},{64,0},{1,65},{65,1},{2,66},{66,2},{3,67},{67,3},{4,68},{68... | collective-permute-start | bytes 1572872 | tf_op jit(solution)/shard_map/ppermute | solution.py:457
  53.8 18.6 %all-to-all-start.1 = ((f32[128,4,128]{2,1,0:T(4,128)}), f32[128,4,128]{2,1,0:T(4,128)S(1)}, u32[]{:S(2)}, u32[]{:S(2)}) async-start(f32[128,4,128]{2,1,0:T(4,128)} %bitcast.3), calls=%async_computation.1 | async-start | bytes 524288 | tf_op jit(solution)/shard_map/all_to_all | solution.py:459
  59.9 30.0 %collective-permute-start.2 = (bf16[2,256,256]{2,1,0:T(8,128)(2,1)}, bf16[2,256,256]{2,1,0:T(8,128)(2,1)S(1)}, u32[]{:S(2)}, u32[]{:S(2)}) collective-permute-start(bf16[2,256,256]{2,1,0:T(8,128)(2,1)} %get-tuple-element.22), channel_id=1, source_target_pairs={{0,64},{64,0},{1,65},{65,1},{2,66},{66,2},{3,67},{67,3},{4,68},{68... | collective-permute-start | bytes 786440 | tf_op jit(solution)/shard_map/ppermute | solution.py:458
  63.3 26.7 %collective-permute-start = (bf16[2,256,256]{2,1,0:T(8,128)(2,1)S(1)}, bf16[2,256,256]{2,1,0:T(8,128)(2,1)S(1)}, u32[]{:S(2)}, u32[]{:S(2)}) collective-permute-start(bf16[2,256,256]{2,1,0:T(8,128)(2,1)S(1)} %get-tuple-element.20), channel_id=1, source_target_pairs={{0,64},{64,0},{1,65},{65,1},{2,66},{66,2},{3,67},{67,3},{4,68},{68... | collective-permute-start | bytes 786440 | tf_op jit(solution)/shard_map/ppermute | solution.py:456

commit v3 on v2

--- a/solution.py
+++ b/solution.py
@@ -21,7 +21,7 @@
 COLS = NCOL // DEVICES
 HALF = NROW // GROUPS
 WIDE = RANK * GROUPS * COLS
-THIRD = 2
+FIRST = 3
 CHUNKS = 4
 CHUNK = SLOTS // CHUNKS
 PLANE = DEVICES * COLS + 1
@@ -39,7 +39,7 @@
 
 
 SIN_FIT = fit(lambda x: np.sin(x) / x, 6)
-COS_FIT = fit(np.cos, 7)
+COS_FIT = fit(np.cos, 6)
 
 
 def tables(length):
@@ -235,34 +235,21 @@
     return jnp.where(group == 0, low, high), jnp.where(group == 0, high, low)
 
 
-def focal_kernel(group_ref, pieces_ref, table_ref, keep_ref, send_ref, real_ref, cross_ref):
-    focal = focal_column(pieces_ref, table_ref, 0)
-    turned = [focal[part].T for part in range(2)]
-    for part in range(2):
-        keep_ref[part], send_ref[part] = split(group_ref[0], turned[part])
-    zero = jnp.zeros((STACK, STACK), jnp.float32)
-    real_ref[...], cross_ref[...] = add_gram(focal, turned, zero, zero)
-
-
-def more_focal_kernel(
-    group_ref, pieces_ref, table_ref, real_ref, cross_ref, keep_ref, second_ref, third_hbm, gram_ref,
-    third_ref, third_sem,
+def focal_kernel(
+    group_ref, pieces_ref, table_ref, keep_ref, first_ref, second_ref, gram_ref
 ):
-    real, cross = real_ref[...], cross_ref[...]
-    for i in range(1, COLS):
+    real = jnp.zeros((STACK, STACK), jnp.float32)
+    cross = jnp.zeros((STACK, STACK), jnp.float32)
+    for i in range(COLS):
         focal = focal_column(pieces_ref, table_ref, i)
         turned = [focal[part].T for part in range(2)]
         for part in range(2):
-            at = (i - 1) * 2 + part
-            kept, sent = split(group_ref[0], turned[part])
-            keep_ref[at] = kept
-            if at < THIRD:
-                third_ref[at] = sent
+            at = 2 * i + part
+            keep_ref[at], sent = split(group_ref[0], turned[part])
+            if at < FIRST:
+                first_ref[at] = sent
             else:
-                second_ref[at - THIRD] = sent
-        if i * 2 == THIRD:
-            late = pltpu.make_async_copy(third_ref, third_hbm, third_sem)
-            late.start()
+                second_ref[at - FIRST] = sent
         real, cross = add_gram(focal, turned, real, cross)
     imag = cross - cross.T
     row = lax.broadcasted_iota(jnp.int32, (STACK, STACK), 0)
@@ -271,7 +258,6 @@
     for q in range(4):
         top, left = (q // 2) * 128, (q % 2) * 128
         gram_ref[pl.ds(q, 128, stride=4), :] = packed[top : top + 128, left : left + 128]
-    late.wait()
 
 
 def total_kernel(parts_ref, out_ref):
@@ -342,17 +328,16 @@
 
 
 def modes_kernel(
-    group_ref, left_ref, scale_ref, kept_ref, kept_more_ref, first_ref, second_ref, third_ref,
-    out_hbm,    wide_ref, out_ref, out_sem,
+    group_ref, left_ref, scale_ref, kept_ref, first_ref, second_ref, out_hbm,
+       wide_ref, out_ref, out_sem,
 ):
     group = group_ref[0]
     left = left_ref[...]
     scale = scale_ref[...]
     sources = (
-        [kept_ref[part] for part in range(2)] + [kept_more_ref[at] for at in range(2 * COLS - 2)],
-        [first_ref[part] for part in range(2)]
-        + [third_ref[at] for at in range(THIRD)]
-        + [second_ref[at] for at in range(2 * COLS - 2 - THIRD)],
+        [kept_ref[at] for at in range(2 * COLS)],
+        [first_ref[at] for at in range(FIRST)]
+        + [second_ref[at] for at in range(2 * COLS - FIRST)],
     )
     for source in range(2):
         first = jnp.where(group == source, 0, COLS)
@@ -429,33 +414,21 @@
     def focal_shape(count):
         return jax.ShapeDtypeStruct((count, STACK, HALF), jnp.bfloat16)
 
-    row_table = jnp.asarray(row_tables())
-    square = jax.ShapeDtypeStruct((STACK, STACK), jnp.float32)
-    kept, swap_first, real, cross = pl.pallas_call(
+    kept, swap_first, swap_second, gram = pl.pallas_call(
         focal_kernel,
-        out_shape=(focal_shape(2), focal_shape(2), square, square),
+        out_shape=(
+            focal_shape(2 * COLS),
+            focal_shape(FIRST),
+            focal_shape(2 * COLS - FIRST),
+            jax.ShapeDtypeStruct((4 * DEVICES, 128), jnp.float32),
+        ),
         in_specs=[SMEM] + [VMEM] * 2,
         out_specs=(VMEM,) * 4,
         compiler_params=params(12),
         name="focal",
-    )(group, pieces, row_table)
-    kept_more, swap_second, swap_third, gram = pl.pallas_call(
-        more_focal_kernel,
-        out_shape=(
-            focal_shape(2 * COLS - 2),
-            focal_shape(2 * COLS - 2 - THIRD),
-            pltpu.HBM((THIRD, STACK, HALF), jnp.bfloat16),
-            jax.ShapeDtypeStruct((4 * DEVICES, 128), jnp.float32),
-        ),
-        in_specs=[SMEM] + [VMEM] * 4,
-        out_specs=(VMEM, VMEM, HBM, VMEM),
-        scratch_shapes=[pltpu.VMEM((THIRD, STACK, HALF), jnp.bfloat16), pltpu.SemaphoreType.DMA],
-        compiler_params=params(12),
-        name="more_focal",
-    )(group, pieces, row_table, real, cross)
+    )(group, pieces, jnp.asarray(row_tables()))
     swap_first = lax.ppermute(swap_first, "grp", [(0, 1), (1, 0)])
     swap_second = lax.ppermute(swap_second, "grp", [(0, 1), (1, 0)])
-    swap_third = lax.ppermute(swap_third, "grp", [(0, 1), (1, 0)])
     parts = lax.all_to_all(gram.reshape(DEVICES, 4, 128), AXES, 0, 0, tiled=True)
     total = pl.pallas_call(
         total_kernel,
@@ -481,7 +454,7 @@
     coherent_modes = pl.pallas_call(
         modes_kernel,
         out_shape=jax.ShapeDtypeStruct((2, RANK, GROUPS * COLS, HALF), jnp.bfloat16),
-        in_specs=[SMEM] + [VMEM] * 7,
+        in_specs=[SMEM] + [VMEM] * 5,
         out_specs=HBM,
         scratch_shapes=[
             pltpu.VMEM((2 * HALF // 128 * WIDE, 128), jnp.float32),
@@ -490,7 +463,7 @@
         ],
         compiler_params=params(16),
         name="modes",
-    )(group, left, scale, kept, kept_more, swap_first, swap_second, swap_third)
+    )(group, left, scale, kept, swap_first, swap_second)
     return coherent_modes, power.reshape(RANK)
 
 

time: 92.1 us -> 95.7 us (1.039)
  waiting for transfers between devices: 9.07 us -> 12 us
    ppermute x1 -> x0, starting transfers between devices: 3.33 us -> none  [local(): swap_third = lax.ppermute(swap_third, 'grp', [(0, 1), (1, 0)])]
    ppermute x1, starting transfers between devices: 0.09 us -> 3.33 us  [local(): swap_first = lax.ppermute(swap_first, 'grp', [(0, 1), (1, 0)])]
    all_to_all x1, waiting for transfers between devices: 9.07 us -> 12 us  [local(): lax.all_to_all(gram.reshape(DEVICES, 4, 128), AXES, 0, 0, tiled=True)]
    pallas_call x2 -> x1, Pallas kernels: 4 us -> 3.7 us  [local(): pl.pallas_call(focal_kernel, out_shape=(focal_shape(2 * COLS), focal_shap...]
  transfers between devices with their start and end apart: 4 -> 3, of which waited for: 1 -> 1; matrix products, arithmetic and copies ran while one was open for 0% -> 0% of each run, Pallas kernels for 3% -> 3%
where the time goes in v3:
time: 95.7 us; the launch traced here: 95.4 us
  blocking collectives  56.5 us (59%)
  Pallas kernels  15 us (16%)
  waiting for transfers between devices  12 us (13%)
  starting transfers between devices  10.6 us (11%)
    all_to_all x1, blocking collectives, local(): pieces = lax.all_to_all(across, AXES, 0, 0, tiled=True)  41.4 us
    all_to_all x1, blocking collectives, local(): lax.all_to_all(total.reshape(DEVICES, 4, 128), AXES, 0, 0, tiled=True)  15.1 us
    all_to_all x1, waiting for transfers between devices, local(): lax.all_to_all(gram.reshape(DEVICES, 4, 128), AXES, 0, 0, tiled=True)  12 us
    pallas_call x1, Pallas kernels, local(): pl.pallas_call(spectra_kernel, out_shape=jax.ShapeDtypeStruct((DEVICES, C...  6.36 us
    all_to_all x1, starting transfers between devices, local(): lax.all_to_all(gram.reshape(DEVICES, 4, 128), AXES, 0, 0, tiled=True)  6.11 us
    pallas_call x1, Pallas kernels, local(): pl.pallas_call(focal_kernel, out_shape=(focal_shape(2 * COLS), focal_shap...  3.7 us
    ppermute x1, starting transfers between devices, local(): swap_first = lax.ppermute(swap_first, 'grp', [(0, 1), (1, 0)])  3.33 us
    pallas_call x1, Pallas kernels, local(): pl.pallas_call(power_kernel, out_shape=(jax.ShapeDtypeStruct((2 * RANK, 2...  2.94 us
  transfers between devices with their start and end apart: 3, of which 1 were waited for; matrix products, arithmetic and copies ran while one was open for 0% of the time, Pallas kernels for 3%

profile of v3, /device:TPU:1, one launch (start us, length us, event | category | flops | bytes accessed | tf_op | source)
XLA Modules:
  0.0 95.4 jit_solution(16363422535519714678)
XLA Ops:
  0.6 6.4 %spectra.1 = bf16[128,4,16,128]{3,2,1,0:T(8,128)(2,1)S(1)} custom-call(s32[1]{0:T(128)} %bitcast.group_ref, s32[256]{0:T(256)} %assign_hbm.1, f32[256]{0:T(256)} %occ_hbm.1, f32[256]{0:T(256)} %chrom_hbm.1, bf16[2,128,8,512]{3,2,1,0:T(8,128)(2,1)} %bitcast.12, f32[8,512]{1,0:T(8,128)} %lens_hbm.1, bf16[2,512,512]{2,1,0:T(8,128)(2,1)} %constant.10.clone.table_hbm), custom_call_target="tpu_custom_call" | custom-call | tf_op jit(solution)/shard_map/spectra/pallas_call | solution.py:380
  7.0 0.0 copy-start
  7.0 41.4 %all_to_all.15 = bf16[128,4,16,128]{3,2,1,0:T(8,128)(2,1)S(1)} all-to-all(bf16[128,4,16,128]{3,2,1,0:T(8,128)(2,1)S(1)} %spectra.1), channel_id=1, replica_groups=mesh['grp'=2,'pix'=64] {'grp','pix'}, dimensions={0} | all-to-all | bytes 4194304 | tf_op jit(solution)/shard_map/all_to_all | solution.py:410
  48.4 0.0 copy-done
  48.4 0.0 copy-start.1
  48.4 3.7 %focal.1 = (bf16[8,256,256]{2,1,0:T(8,128)(2,1)S(1)}, bf16[3,256,256]{2,1,0:T(8,128)(2,1)S(1)}, bf16[5,256,256]{2,1,0:T(8,128)(2,1)S(1)}, f32[512,128]{1,0:T(8,128)}) custom-call(s32[1]{0:T(128)} %bitcast.group_ref, bf16[128,4,2,8,128]{4,3,2,1,0:T(8,128)(2,1)S(1)} %bitcast.8, bf16[2,512,512]{2,1,0:T(8,128)(2,1)S(1)} %copy-done), custom_call_target="tpu_custom_call" | custom-call | tf_op jit(solution)/shard_map/focal/pallas_call | solution.py:417
  52.1 0.0 copy-start.2
  52.1 0.7 copy-done.2
  52.9 1.1 %collective-permute-start.1 = (bf16[5,256,256]{2,1,0:T(8,128)(2,1)S(1)}, bf16[5,256,256]{2,1,0:T(8,128)(2,1)S(1)}, u32[]{:S(2)}, u32[]{:S(2)}) collective-permute-start(bf16[5,256,256]{2,1,0:T(8,128)(2,1)S(1)} %get-tuple-element.14), channel_id=1, source_target_pairs={{0,64},{64,0},{1,65},{65,1},{2,66},{66,2},{3,67},{67,3},{4,68},{68... | collective-permute-start | bytes 1966088 | tf_op jit(solution)/shard_map/ppermute | solution.py:431
  54.0 6.1 %all-to-all-start.1 = ((f32[128,4,128]{2,1,0:T(4,128)}), f32[128,4,128]{2,1,0:T(4,128)S(1)}, u32[]{:S(2)}, u32[]{:S(2)}) async-start(f32[128,4,128]{2,1,0:T(4,128)} %bitcast.3), calls=%async_computation.1 | async-start | bytes 524288 | tf_op jit(solution)/shard_map/all_to_all | solution.py:432
  60.1 3.3 %collective-permute-start = (bf16[3,256,256]{2,1,0:T(8,128)(2,1)}, bf16[3,256,256]{2,1,0:T(8,128)(2,1)S(1)}, u32[]{:S(2)}, u32[]{:S(2)}) collective-permute-start(bf16[3,256,256]{2,1,0:T(8,128)(2,1)} %copy-done.2), channel_id=1, source_target_pairs={{0,64},{64,0},{1,65},{65,1},{2,66},{66,2},{3,67},{67,3},{4,68},{68... | collective-permute-start | bytes 1179656 | tf_op jit(solution)/shard_map/ppermute | solution.py:430
  63.4 12.0 %all-to-all-done.1 = f32[128,4,128]{2,1,0:T(4,128)S(1)} async-done(((f32[128,4,128]{2,1,0:T(4,128)}), f32[128,4,128]{2,1,0:T(4,128)S(1)}, u32[]{:S(2)}, u32[]{:S(2)}) %all-to-all-start.1) | async-done | bytes 262176 | tf_op jit(solution)/shard_map/all_to_all | solution.py:432
  75.4 0.1 total.1
  75.5 15.1 %all_to_all.16 = f32[128,4,128]{2,1,0:T(4,128)S(1)} all-to-all(f32[128,4,128]{2,1,0:T(4,128)S(1)} %bitcast.11), channel_id=1, replica_groups=mesh['grp'=2,'pix'=64] {'grp','pix'}, dimensions={0} | all-to-all | bytes 524288 | tf_op jit(solution)/shard_map/all_to_all | solution.py:441
  90.6 0.0 copy-done.1
  90.6 2.9 %power.1 = (bf16[256,512]{1,0:T(8,128)(2,1)S(1)}, f32[128,128]{1,0:T(8,128)S(1)}, f32[1,128]{1,0:T(1,128)}) custom-call(f32[512,128]{1,0:T(8,128)S(1)} %bitcast.10, f32[2,256,128]{2,1,0:T(8,128)S(1)} %copy-done.1), custom_call_target="tpu_custom_call" | custom-call | tf_op jit(solution)/shard_map/power/pallas_call | solution.py:442
  93.5 0.0 collective-permute-done.first_ref
  93.5 0.0 collective-permute-done.1.second_ref
  93.5 1.9 %modes.1 = bf16[2,128,8,256]{3,2,1,0:T(8,128)(2,1)} custom-call(s32[1]{0:T(128)} %bitcast.group_ref, bf16[256,512]{1,0:T(8,128)(2,1)S(1)} %get-tuple-element.10.left_ref, f32[128,128]{1,0:T(8,128)S(1)} %get-tuple-element.11.scale_ref, bf16[8,256,256]{2,1,0:T(8,128)(2,1)S(1)} %get-tuple-element.12.kept_ref, ...), custom_call_target="tpu_custom_call" | custom-call | tf_op jit(solution)/shard_map/modes/pallas_call | solution.py:454
Async XLA Ops:
  7.0 41.4 %copy-start = (bf16[2,512,512]{2,1,0:T(8,128)(2,1)S(1)}, bf16[2,512,512]{2,1,0:T(8,128)(2,1)}, u32[]{:S(2)}) copy-start(bf16[2,512,512]{2,1,0:T(8,128)(2,1)} %constant.11.clone.table_ref) | copy-start | bytes 3145732
  48.4 42.2 %copy-start.1 = (f32[2,256,128]{2,1,0:T(8,128)S(1)}, f32[2,256,128]{2,1,0:T(8,128)}, u32[]{:S(2)}) copy-start(f32[2,256,128]{2,1,0:T(8,128)} %start_ref.1) | copy-start | bytes 786436
  52.1 0.7 copy-start.2
  52.9 40.7 %collective-permute-start.1 = (bf16[5,256,256]{2,1,0:T(8,128)(2,1)S(1)}, bf16[5,256,256]{2,1,0:T(8,128)(2,1)S(1)}, u32[]{:S(2)}, u32[]{:S(2)}) collective-permute-start(bf16[5,256,256]{2,1,0:T(8,128)(2,1)S(1)} %get-tuple-element.14), channel_id=1, source_target_pairs={{0,64},{64,0},{1,65},{65,1},{2,66},{66,2},{3,67},{67,3},{4,68},{68... | collective-permute-start | bytes 1966088 | tf_op jit(solution)/shard_map/ppermute | solution.py:431
  54.0 21.4 %all-to-all-start.1 = ((f32[128,4,128]{2,1,0:T(4,128)}), f32[128,4,128]{2,1,0:T(4,128)S(1)}, u32[]{:S(2)}, u32[]{:S(2)}) async-start(f32[128,4,128]{2,1,0:T(4,128)} %bitcast.3), calls=%async_computation.1 | async-start | bytes 524288 | tf_op jit(solution)/shard_map/all_to_all | solution.py:432
  60.1 33.4 %collective-permute-start = (bf16[3,256,256]{2,1,0:T(8,128)(2,1)}, bf16[3,256,256]{2,1,0:T(8,128)(2,1)S(1)}, u32[]{:S(2)}, u32[]{:S(2)}) collective-permute-start(bf16[3,256,256]{2,1,0:T(8,128)(2,1)} %copy-done.2), channel_id=1, source_target_pairs={{0,64},{64,0},{1,65},{65,1},{2,66},{66,2},{3,67},{67,3},{4,68},{68... | collective-permute-start | bytes 1179656 | tf_op jit(solution)/shard_map/ppermute | solution.py:430

commit v4 on v3

--- a/solution.py
+++ b/solution.py
@@ -27,19 +27,23 @@
 PLANE = DEVICES * COLS + 1
 AXES = ("grp", "pix")
 
-LIMIT = 0.5 * 1.5 * 3.140625
-
-
-def fit(function, terms):
-    limit = LIMIT * 1.001
+LENS = 3.140625
+SCALE_LOW, SCALE_HIGH = 0.5, 1.5
+STEP = 0.125
+BASES = int((SCALE_HIGH - SCALE_LOW) / STEP) + 1
+
+
+def fit(function, terms, limit):
     nodes = np.cos(np.pi * (np.arange(400) + 0.5) / 400)
-    square = (nodes + 1.0) * 0.5 * limit * limit
+    square = (nodes + 1.0) * 0.5 * (limit * 1.001) ** 2
     powers = np.stack([square**k for k in range(terms)], axis=1)
     return [float(c) for c in np.linalg.lstsq(powers, function(np.sqrt(square)), rcond=None)[0]]
 
 
-SIN_FIT = fit(lambda x: np.sin(x) / x, 6)
-COS_FIT = fit(np.cos, 6)
+SIN_FIT = fit(lambda x: np.sin(x) / x, 6, 0.5 * SCALE_HIGH * LENS)
+COS_FIT = fit(np.cos, 7, 0.5 * SCALE_HIGH * LENS)
+SIN_REST = fit(lambda x: np.sin(x) / x, 3, 0.5 * STEP * LENS)
+COS_REST = fit(np.cos, 3, 0.5 * STEP * LENS)
 
 
 def tables(length):
@@ -91,7 +95,7 @@
 def spectra_kernel(
     group_ref, assign_hbm, occ_hbm, chrom_hbm, fields_hbm, lens_hbm, table_hbm, out_ref,
     assign_ref, occ_ref, chrom_ref, fields_ref, lens_ref, table_ref,
-    real_ref, imag_ref, wide_ref, small_sem, field_sem, table_sem,
+    base_ref, real_ref, imag_ref, wide_ref, small_sem, field_sem, table_sem,
 ):
     def chunk(part, c):
         slots = pl.ds(c * CHUNK, CHUNK)
@@ -125,19 +129,37 @@
         copy.wait()
     base = group_ref[0] * SLOTS
 
+    def base_wave(k, carry):
+        scale = 0.5 * (SCALE_LOW + STEP * k.astype(jnp.float32))
+        for lane in range(NCOL // 128):
+            cut = pl.ds(lane * 128, 128)
+            half = lens_ref[:, cut] * scale
+            square = half * half
+            sine_half = half * polynomial(square, SIN_FIT)
+            double = sine_half + sine_half
+            base_ref[k, 0, :, cut] = 1.0 - double * sine_half
+            base_ref[k, 1, :, cut] = double * polynomial(square, COS_FIT)
+        return carry
+
+    lax.fori_loop(0, BASES, base_wave, 0)
+
     def phase(m, carry):
         electron = assign_ref[base + m]
         amplitude = jnp.sqrt(jnp.full((ROWS, 128), occ_ref[electron], jnp.float32))
-        twice = amplitude + amplitude
-        chromatic = chrom_ref[electron] * 0.5
+        chromatic = chrom_ref[electron]
+        nearest = ((chromatic - SCALE_LOW) * (1.0 / STEP) + 0.5).astype(jnp.int32)
+        nearest = jnp.clip(nearest, 0, BASES - 1)
+        rest = chromatic - (SCALE_LOW + STEP * nearest.astype(jnp.float32))
         for lane in range(NCOL // 128):
             cut = pl.ds(lane * 128, 128)
-            half = lens_ref[:, cut] * chromatic
-            square = half * half
-            sine_half = half * polynomial(square, SIN_FIT)
-            scaled = sine_half * twice
-            sine = scaled * polynomial(square, COS_FIT)
-            cosine = amplitude - scaled * sine_half
+            angle = lens_ref[:, cut] * rest
+            square = angle * angle
+            sine_rest = amplitude * (angle * polynomial(square, SIN_REST))
+            cosine_rest = amplitude * polynomial(square, COS_REST)
+            cosine_base = base_ref[nearest, 0, :, cut]
+            sine_base = base_ref[nearest, 1, :, cut]
+            cosine = cosine_base * cosine_rest - sine_base * sine_rest
+            sine = sine_base * cosine_rest + cosine_base * sine_rest
             field_re = fields_ref[0, m, :, cut].astype(jnp.float32)
             field_im = fields_ref[1, m, :, cut].astype(jnp.float32)
             rows = pl.ds(pl.multiple_of(lane * ROWS * SLOTS + m * ROWS, ROWS), ROWS)
@@ -201,7 +223,7 @@
             out_ref[d, i] = rows.astype(jnp.bfloat16)
             return carry
 
-        lax.fori_loop(0, DEVICES, gather, 0, unroll=8)
+        lax.fori_loop(0, DEVICES, gather, 0, unroll=DEVICES)
 
 
 def focal_column(pieces_ref, table_ref, i):
@@ -389,6 +411,7 @@
             pltpu.VMEM((2, SLOTS, ROWS, NCOL), jnp.bfloat16),
             pltpu.VMEM((ROWS, NCOL), jnp.float32),
             pltpu.VMEM((2, NCOL, NCOL), jnp.bfloat16),
+            pltpu.VMEM((BASES, 2, ROWS, NCOL), jnp.float32),
             pltpu.VMEM((NCOL // 128 * ROWS * SLOTS, 128), jnp.float32),
             pltpu.VMEM((NCOL // 128 * ROWS * SLOTS, 128), jnp.float32),
             pltpu.VMEM((2 * ROWS * PLANE, SLOTS), jnp.float32),

time: 95.7 us -> 95.2 us (level)
  no operation moved by 1% of the time
where the time goes in v4:
time: 95.2 us; the launch traced here: 95 us
  blocking collectives  56.5 us (59%)
  Pallas kernels  14.6 us (15%)
  waiting for transfers between devices  12 us (13%)
  starting transfers between devices  10.6 us (11%)
    all_to_all x1, blocking collectives, local(): pieces = lax.all_to_all(across, AXES, 0, 0, tiled=True)  41.4 us
    all_to_all x1, blocking collectives, local(): lax.all_to_all(total.reshape(DEVICES, 4, 128), AXES, 0, 0, tiled=True)  15.1 us
    all_to_all x1, waiting for transfers between devices, local(): lax.all_to_all(gram.reshape(DEVICES, 4, 128), AXES, 0, 0, tiled=True)  12 us
    all_to_all x1, starting transfers between devices, local(): lax.all_to_all(gram.reshape(DEVICES, 4, 128), AXES, 0, 0, tiled=True)  6.11 us
    pallas_call x1, Pallas kernels, local(): pl.pallas_call(spectra_kernel, out_shape=jax.ShapeDtypeStruct((DEVICES, C...  5.93 us
    pallas_call x1, Pallas kernels, local(): pl.pallas_call(focal_kernel, out_shape=(focal_shape(2 * COLS), focal_shap...  3.71 us
    ppermute x1, starting transfers between devices, local(): swap_first = lax.ppermute(swap_first, 'grp', [(0, 1), (1, 0)])  3.33 us
    pallas_call x1, Pallas kernels, local(): pl.pallas_call(power_kernel, out_shape=(jax.ShapeDtypeStruct((2 * RANK, 2...  2.94 us
  transfers between devices with their start and end apart: 3, of which 1 were waited for; matrix products, arithmetic and copies ran while one was open for 0% of the time, Pallas kernels for 3%

profile of v4, /device:TPU:1, one launch (start us, length us, event | category | flops | bytes accessed | tf_op | source)
XLA Modules:
  0.0 95.0 jit_solution(778892222012021560)
XLA Ops:
  0.6 5.9 %spectra.1 = bf16[128,4,16,128]{3,2,1,0:T(8,128)(2,1)S(1)} custom-call(s32[1]{0:T(128)} %bitcast.group_ref, s32[256]{0:T(256)} %assign_hbm.1, f32[256]{0:T(256)} %occ_hbm.1, f32[256]{0:T(256)} %chrom_hbm.1, bf16[2,128,8,512]{3,2,1,0:T(8,128)(2,1)} %bitcast.12, f32[8,512]{1,0:T(8,128)} %lens_hbm.1, bf16[2,512,512]{2,1,0:T(8,128)(2,1)} %constant.10.clone.table_hbm), custom_call_target="tpu_custom_call" | custom-call | tf_op jit(solution)/shard_map/spectra/pallas_call | solution.py:402
  6.6 0.0 copy-start
  6.6 41.4 %all_to_all.15 = bf16[128,4,16,128]{3,2,1,0:T(8,128)(2,1)S(1)} all-to-all(bf16[128,4,16,128]{3,2,1,0:T(8,128)(2,1)S(1)} %spectra.1), channel_id=1, replica_groups=mesh['grp'=2,'pix'=64] {'grp','pix'}, dimensions={0} | all-to-all | bytes 4194304 | tf_op jit(solution)/shard_map/all_to_all | solution.py:433
  48.0 0.0 copy-done
  48.0 0.0 copy-start.1
  48.0 3.7 %focal.1 = (bf16[8,256,256]{2,1,0:T(8,128)(2,1)S(1)}, bf16[3,256,256]{2,1,0:T(8,128)(2,1)S(1)}, bf16[5,256,256]{2,1,0:T(8,128)(2,1)S(1)}, f32[512,128]{1,0:T(8,128)}) custom-call(s32[1]{0:T(128)} %bitcast.group_ref, bf16[128,4,2,8,128]{4,3,2,1,0:T(8,128)(2,1)S(1)} %bitcast.8, bf16[2,512,512]{2,1,0:T(8,128)(2,1)S(1)} %copy-done), custom_call_target="tpu_custom_call" | custom-call | tf_op jit(solution)/shard_map/focal/pallas_call | solution.py:440
  51.7 0.0 copy-start.2
  51.7 0.7 copy-done.2
  52.4 1.1 %collective-permute-start.1 = (bf16[5,256,256]{2,1,0:T(8,128)(2,1)S(1)}, bf16[5,256,256]{2,1,0:T(8,128)(2,1)S(1)}, u32[]{:S(2)}, u32[]{:S(2)}) collective-permute-start(bf16[5,256,256]{2,1,0:T(8,128)(2,1)S(1)} %get-tuple-element.14), channel_id=1, source_target_pairs={{0,64},{64,0},{1,65},{65,1},{2,66},{66,2},{3,67},{67,3},{4,68},{68... | collective-permute-start | bytes 1966088 | tf_op jit(solution)/shard_map/ppermute | solution.py:454
  53.6 6.1 %all-to-all-start.1 = ((f32[128,4,128]{2,1,0:T(4,128)}), f32[128,4,128]{2,1,0:T(4,128)S(1)}, u32[]{:S(2)}, u32[]{:S(2)}) async-start(f32[128,4,128]{2,1,0:T(4,128)} %bitcast.3), calls=%async_computation.1 | async-start | bytes 524288 | tf_op jit(solution)/shard_map/all_to_all | solution.py:455
  59.7 3.3 %collective-permute-start = (bf16[3,256,256]{2,1,0:T(8,128)(2,1)}, bf16[3,256,256]{2,1,0:T(8,128)(2,1)S(1)}, u32[]{:S(2)}, u32[]{:S(2)}) collective-permute-start(bf16[3,256,256]{2,1,0:T(8,128)(2,1)} %copy-done.2), channel_id=1, source_target_pairs={{0,64},{64,0},{1,65},{65,1},{2,66},{66,2},{3,67},{67,3},{4,68},{68... | collective-permute-start | bytes 1179656 | tf_op jit(solution)/shard_map/ppermute | solution.py:453
  63.0 12.0 %all-to-all-done.1 = f32[128,4,128]{2,1,0:T(4,128)S(1)} async-done(((f32[128,4,128]{2,1,0:T(4,128)}), f32[128,4,128]{2,1,0:T(4,128)S(1)}, u32[]{:S(2)}, u32[]{:S(2)}) %all-to-all-start.1) | async-done | bytes 262176 | tf_op jit(solution)/shard_map/all_to_all | solution.py:455
  75.0 0.1 total.1
  75.1 15.1 %all_to_all.16 = f32[128,4,128]{2,1,0:T(4,128)S(1)} all-to-all(f32[128,4,128]{2,1,0:T(4,128)S(1)} %bitcast.11), channel_id=1, replica_groups=mesh['grp'=2,'pix'=64] {'grp','pix'}, dimensions={0} | all-to-all | bytes 524288 | tf_op jit(solution)/shard_map/all_to_all | solution.py:464
  90.2 0.0 copy-done.1
  90.2 2.9 %power.1 = (bf16[256,512]{1,0:T(8,128)(2,1)S(1)}, f32[128,128]{1,0:T(8,128)S(1)}, f32[1,128]{1,0:T(1,128)}) custom-call(f32[512,128]{1,0:T(8,128)S(1)} %bitcast.10, f32[2,256,128]{2,1,0:T(8,128)S(1)} %copy-done.1), custom_call_target="tpu_custom_call" | custom-call | tf_op jit(solution)/shard_map/power/pallas_call | solution.py:465
  93.1 0.0 collective-permute-done.first_ref
  93.1 0.0 collective-permute-done.1.second_ref
  93.1 1.9 %modes.1 = bf16[2,128,8,256]{3,2,1,0:T(8,128)(2,1)} custom-call(s32[1]{0:T(128)} %bitcast.group_ref, bf16[256,512]{1,0:T(8,128)(2,1)S(1)} %get-tuple-element.10.left_ref, f32[128,128]{1,0:T(8,128)S(1)} %get-tuple-element.11.scale_ref, bf16[8,256,256]{2,1,0:T(8,128)(2,1)S(1)} %get-tuple-element.12.kept_ref, ...), custom_call_target="tpu_custom_call" | custom-call | tf_op jit(solution)/shard_map/modes/pallas_call | solution.py:477
Async XLA Ops:
  6.6 41.4 %copy-start = (bf16[2,512,512]{2,1,0:T(8,128)(2,1)S(1)}, bf16[2,512,512]{2,1,0:T(8,128)(2,1)}, u32[]{:S(2)}) copy-start(bf16[2,512,512]{2,1,0:T(8,128)(2,1)} %constant.11.clone.table_ref) | copy-start | bytes 3145732
  48.0 42.2 %copy-start.1 = (f32[2,256,128]{2,1,0:T(8,128)S(1)}, f32[2,256,128]{2,1,0:T(8,128)}, u32[]{:S(2)}) copy-start(f32[2,256,128]{2,1,0:T(8,128)} %start_ref.1) | copy-start | bytes 786436
  51.7 0.7 copy-start.2
  52.4 40.7 %collective-permute-start.1 = (bf16[5,256,256]{2,1,0:T(8,128)(2,1)S(1)}, bf16[5,256,256]{2,1,0:T(8,128)(2,1)S(1)}, u32[]{:S(2)}, u32[]{:S(2)}) collective-permute-start(bf16[5,256,256]{2,1,0:T(8,128)(2,1)S(1)} %get-tuple-element.14), channel_id=1, source_target_pairs={{0,64},{64,0},{1,65},{65,1},{2,66},{66,2},{3,67},{67,3},{4,68},{68... | collective-permute-start | bytes 1966088 | tf_op jit(solution)/shard_map/ppermute | solution.py:454
  53.6 21.4 %all-to-all-start.1 = ((f32[128,4,128]{2,1,0:T(4,128)}), f32[128,4,128]{2,1,0:T(4,128)S(1)}, u32[]{:S(2)}, u32[]{:S(2)}) async-start(f32[128,4,128]{2,1,0:T(4,128)} %bitcast.3), calls=%async_computation.1 | async-start | bytes 524288 | tf_op jit(solution)/shard_map/all_to_all | solution.py:455
  59.7 33.4 %collective-permute-start = (bf16[3,256,256]{2,1,0:T(8,128)(2,1)}, bf16[3,256,256]{2,1,0:T(8,128)(2,1)S(1)}, u32[]{:S(2)}, u32[]{:S(2)}) collective-permute-start(bf16[3,256,256]{2,1,0:T(8,128)(2,1)} %copy-done.2), channel_id=1, source_target_pairs={{0,64},{64,0},{1,65},{65,1},{2,66},{66,2},{3,67},{67,3},{4,68},{68... | collective-permute-start | bytes 1179656 | tf_op jit(solution)/shard_map/ppermute | solution.py:453

commit v5 on v4

--- a/solution.py
+++ b/solution.py
@@ -22,7 +22,8 @@
 HALF = NROW // GROUPS
 WIDE = RANK * GROUPS * COLS
 FIRST = 3
-CHUNKS = 4
+SENDS = 4
+CHUNKS = 2
 CHUNK = SLOTS // CHUNKS
 PLANE = DEVICES * COLS + 1
 AXES = ("grp", "pix")
@@ -329,8 +330,9 @@
         norm = jnp.sqrt(
             jnp.sum(image_re * image_re + image_im * image_im, axis=0, keepdims=True) + 1e-06
         )
-        basis_re = image_re / norm
-        basis_im = image_im / norm
+        inverse = 1.0 / norm
+        basis_re = image_re * inverse
+        basis_im = image_im * inverse
     rounded_re = basis_re.astype(jnp.bfloat16)
     rounded_im = basis_im.astype(jnp.bfloat16)
     image_re, image_im = apply(rounded_re, rounded_im)
@@ -375,13 +377,22 @@
                         mode[part * RANK : (part + 1) * RANK, lane * 128 : (lane + 1) * 128] * scale
                     )
     copies = []
-    for part in range(2):
+    for piece in range(2 * SENDS):
+        part, modes = piece // SENDS, RANK // SENDS
+        first = piece % SENDS * modes
         for lane in range(HALF // 128):
-            at = (part * 2 + lane) * WIDE
-            out_ref[part, :, :, lane * 128 : (lane + 1) * 128] = (
-                wide_ref[at : at + WIDE, :].reshape(RANK, GROUPS * COLS, 128).astype(jnp.bfloat16)
+            at = (part * 2 + lane) * WIDE + first * GROUPS * COLS
+            out_ref[part, first : first + modes, :, lane * 128 : (lane + 1) * 128] = (
+                wide_ref[at : at + modes * GROUPS * COLS, :]
+                .reshape(modes, GROUPS * COLS, 128)
+                .astype(jnp.bfloat16)
             )
-        copies.append(pltpu.make_async_copy(out_ref.at[part], out_hbm.at[part], out_sem.at[part]))
+        rows = pl.ds(first, modes)
+        copies.append(
+            pltpu.make_async_copy(
+                out_ref.at[part, rows], out_hbm.at[part, rows], out_sem.at[piece]
+            )
+        )
         copies[-1].start()
     for copy in copies:
         copy.wait()
@@ -482,7 +493,7 @@
         scratch_shapes=[
             pltpu.VMEM((2 * HALF // 128 * WIDE, 128), jnp.float32),
             pltpu.VMEM((2, RANK, GROUPS * COLS, HALF), jnp.bfloat16),
-            pltpu.SemaphoreType.DMA((2,)),
+            pltpu.SemaphoreType.DMA((2 * SENDS,)),
         ],
         compiler_params=params(16),
         name="modes",

time: 95.2 us -> 95 us (level)
  no operation moved by 1% of the time
where the time goes in v5:
time: 95 us; the launch traced here: 94.8 us
  blocking collectives  56.4 us (59%)
  Pallas kernels  14.4 us (15%)
  waiting for transfers between devices  12 us (13%)
  starting transfers between devices  10.6 us (11%)
    all_to_all x1, blocking collectives, local(): pieces = lax.all_to_all(across, AXES, 0, 0, tiled=True)  41.4 us
    all_to_all x1, blocking collectives, local(): lax.all_to_all(total.reshape(DEVICES, 4, 128), AXES, 0, 0, tiled=True)  15.1 us
    all_to_all x1, waiting for transfers between devices, local(): lax.all_to_all(gram.reshape(DEVICES, 4, 128), AXES, 0, 0, tiled=True)  12 us
    all_to_all x1, starting transfers between devices, local(): lax.all_to_all(gram.reshape(DEVICES, 4, 128), AXES, 0, 0, tiled=True)  6.1 us
    pallas_call x1, Pallas kernels, local(): pl.pallas_call(spectra_kernel, out_shape=jax.ShapeDtypeStruct((DEVICES, C...  5.81 us
    pallas_call x1, Pallas kernels, local(): pl.pallas_call(focal_kernel, out_shape=(focal_shape(2 * COLS), focal_shap...  3.7 us
    ppermute x1, starting transfers between devices, local(): swap_first = lax.ppermute(swap_first, 'grp', [(0, 1), (1, 0)])  3.33 us
    pallas_call x1, Pallas kernels, local(): pl.pallas_call(power_kernel, out_shape=(jax.ShapeDtypeStruct((2 * RANK, 2...  2.94 us
  transfers between devices with their start and end apart: 3, of which 1 were waited for; matrix products, arithmetic and copies ran while one was open for 0% of the time, Pallas kernels for 3%

profile of v5, /device:TPU:1, one launch (start us, length us, event | category | flops | bytes accessed | tf_op | source)
XLA Modules:
  0.0 94.8 jit_solution(6142692740820337834)
XLA Ops:
  0.6 5.8 %spectra.1 = bf16[128,4,16,128]{3,2,1,0:T(8,128)(2,1)S(1)} custom-call(s32[1]{0:T(128)} %bitcast.group_ref, s32[256]{0:T(256)} %assign_hbm.1, f32[256]{0:T(256)} %occ_hbm.1, f32[256]{0:T(256)} %chrom_hbm.1, bf16[2,128,8,512]{3,2,1,0:T(8,128)(2,1)} %bitcast.12, f32[8,512]{1,0:T(8,128)} %lens_hbm.1, bf16[2,512,512]{2,1,0:T(8,128)(2,1)} %constant.10.clone.table_hbm), custom_call_target="tpu_custom_call" | custom-call | tf_op jit(solution)/shard_map/spectra/pallas_call | solution.py:413
  6.5 0.0 copy-start
  6.5 41.4 %all_to_all.15 = bf16[128,4,16,128]{3,2,1,0:T(8,128)(2,1)S(1)} all-to-all(bf16[128,4,16,128]{3,2,1,0:T(8,128)(2,1)S(1)} %spectra.1), channel_id=1, replica_groups=mesh['grp'=2,'pix'=64] {'grp','pix'}, dimensions={0} | all-to-all | bytes 4194304 | tf_op jit(solution)/shard_map/all_to_all | solution.py:444
  47.9 0.0 copy-done
  47.9 0.0 copy-start.1
  47.9 3.7 %focal.1 = (bf16[8,256,256]{2,1,0:T(8,128)(2,1)S(1)}, bf16[3,256,256]{2,1,0:T(8,128)(2,1)S(1)}, bf16[5,256,256]{2,1,0:T(8,128)(2,1)S(1)}, f32[512,128]{1,0:T(8,128)}) custom-call(s32[1]{0:T(128)} %bitcast.group_ref, bf16[128,4,2,8,128]{4,3,2,1,0:T(8,128)(2,1)S(1)} %bitcast.8, bf16[2,512,512]{2,1,0:T(8,128)(2,1)S(1)} %copy-done), custom_call_target="tpu_custom_call" | custom-call | tf_op jit(solution)/shard_map/focal/pallas_call | solution.py:451
  51.6 0.0 copy-start.2
  51.6 0.7 copy-done.2
  52.3 1.1 %collective-permute-start.1 = (bf16[5,256,256]{2,1,0:T(8,128)(2,1)S(1)}, bf16[5,256,256]{2,1,0:T(8,128)(2,1)S(1)}, u32[]{:S(2)}, u32[]{:S(2)}) collective-permute-start(bf16[5,256,256]{2,1,0:T(8,128)(2,1)S(1)} %get-tuple-element.14), channel_id=1, source_target_pairs={{0,64},{64,0},{1,65},{65,1},{2,66},{66,2},{3,67},{67,3},{4,68},{68... | collective-permute-start | bytes 1966088 | tf_op jit(solution)/shard_map/ppermute | solution.py:465
  53.5 6.1 %all-to-all-start.1 = ((f32[128,4,128]{2,1,0:T(4,128)}), f32[128,4,128]{2,1,0:T(4,128)S(1)}, u32[]{:S(2)}, u32[]{:S(2)}) async-start(f32[128,4,128]{2,1,0:T(4,128)} %bitcast.3), calls=%async_computation.1 | async-start | bytes 524288 | tf_op jit(solution)/shard_map/all_to_all | solution.py:466
  59.6 3.3 %collective-permute-start = (bf16[3,256,256]{2,1,0:T(8,128)(2,1)}, bf16[3,256,256]{2,1,0:T(8,128)(2,1)S(1)}, u32[]{:S(2)}, u32[]{:S(2)}) collective-permute-start(bf16[3,256,256]{2,1,0:T(8,128)(2,1)} %copy-done.2), channel_id=1, source_target_pairs={{0,64},{64,0},{1,65},{65,1},{2,66},{66,2},{3,67},{67,3},{4,68},{68... | collective-permute-start | bytes 1179656 | tf_op jit(solution)/shard_map/ppermute | solution.py:464
  62.9 12.0 %all-to-all-done.1 = f32[128,4,128]{2,1,0:T(4,128)S(1)} async-done(((f32[128,4,128]{2,1,0:T(4,128)}), f32[128,4,128]{2,1,0:T(4,128)S(1)}, u32[]{:S(2)}, u32[]{:S(2)}) %all-to-all-start.1) | async-done | bytes 262176 | tf_op jit(solution)/shard_map/all_to_all | solution.py:466
  74.9 0.1 total.1
  75.0 15.1 %all_to_all.16 = f32[128,4,128]{2,1,0:T(4,128)S(1)} all-to-all(f32[128,4,128]{2,1,0:T(4,128)S(1)} %bitcast.11), channel_id=1, replica_groups=mesh['grp'=2,'pix'=64] {'grp','pix'}, dimensions={0} | all-to-all | bytes 524288 | tf_op jit(solution)/shard_map/all_to_all | solution.py:475
  90.0 0.0 copy-done.1
  90.0 2.9 %power.1 = (bf16[256,512]{1,0:T(8,128)(2,1)S(1)}, f32[128,128]{1,0:T(8,128)S(1)}, f32[1,128]{1,0:T(1,128)}) custom-call(f32[512,128]{1,0:T(8,128)S(1)} %bitcast.10, f32[2,256,128]{2,1,0:T(8,128)S(1)} %copy-done.1), custom_call_target="tpu_custom_call" | custom-call | tf_op jit(solution)/shard_map/power/pallas_call | solution.py:476
  93.0 0.0 collective-permute-done.first_ref
  93.0 0.0 collective-permute-done.1.second_ref
  93.0 1.9 %modes.1 = bf16[2,128,8,256]{3,2,1,0:T(8,128)(2,1)} custom-call(s32[1]{0:T(128)} %bitcast.group_ref, bf16[256,512]{1,0:T(8,128)(2,1)S(1)} %get-tuple-element.10.left_ref, f32[128,128]{1,0:T(8,128)S(1)} %get-tuple-element.11.scale_ref, bf16[8,256,256]{2,1,0:T(8,128)(2,1)S(1)} %get-tuple-element.12.kept_ref, ...), custom_call_target="tpu_custom_call" | custom-call | tf_op jit(solution)/shard_map/modes/pallas_call | solution.py:488
Async XLA Ops:
  6.5 41.4 %copy-start = (bf16[2,512,512]{2,1,0:T(8,128)(2,1)S(1)}, bf16[2,512,512]{2,1,0:T(8,128)(2,1)}, u32[]{:S(2)}) copy-start(bf16[2,512,512]{2,1,0:T(8,128)(2,1)} %constant.11.clone.table_ref) | copy-start | bytes 3145732
  47.9 42.2 %copy-start.1 = (f32[2,256,128]{2,1,0:T(8,128)S(1)}, f32[2,256,128]{2,1,0:T(8,128)}, u32[]{:S(2)}) copy-start(f32[2,256,128]{2,1,0:T(8,128)} %start_ref.1) | copy-start | bytes 786436
  51.6 0.7 copy-start.2
  52.3 40.7 %collective-permute-start.1 = (bf16[5,256,256]{2,1,0:T(8,128)(2,1)S(1)}, bf16[5,256,256]{2,1,0:T(8,128)(2,1)S(1)}, u32[]{:S(2)}, u32[]{:S(2)}) collective-permute-start(bf16[5,256,256]{2,1,0:T(8,128)(2,1)S(1)} %get-tuple-element.14), channel_id=1, source_target_pairs={{0,64},{64,0},{1,65},{65,1},{2,66},{66,2},{3,67},{67,3},{4,68},{68... | collective-permute-start | bytes 1966088 | tf_op jit(solution)/shard_map/ppermute | solution.py:465
  53.5 21.4 %all-to-all-start.1 = ((f32[128,4,128]{2,1,0:T(4,128)}), f32[128,4,128]{2,1,0:T(4,128)S(1)}, u32[]{:S(2)}, u32[]{:S(2)}) async-start(f32[128,4,128]{2,1,0:T(4,128)} %bitcast.3), calls=%async_computation.1 | async-start | bytes 524288 | tf_op jit(solution)/shard_map/all_to_all | solution.py:466
  59.6 33.4 %collective-permute-start = (bf16[3,256,256]{2,1,0:T(8,128)(2,1)}, bf16[3,256,256]{2,1,0:T(8,128)(2,1)S(1)}, u32[]{:S(2)}, u32[]{:S(2)}) collective-permute-start(bf16[3,256,256]{2,1,0:T(8,128)(2,1)} %copy-done.2), channel_id=1, source_target_pairs={{0,64},{64,0},{1,65},{65,1},{2,66},{66,2},{3,67},{67,3},{4,68},{68... | collective-permute-start | bytes 1179656 | tf_op jit(solution)/shard_map/ppermute | solution.py:464

commit v6 on v4

--- a/solution.py
+++ b/solution.py
@@ -20,7 +20,8 @@
 ROWS = NROW // PIX
 COLS = NCOL // DEVICES
 HALF = NROW // GROUPS
-WIDE = RANK * GROUPS * COLS
+PITCH = RANK + 1
+WIDE = PITCH * GROUPS * COLS
 FIRST = 3
 CHUNKS = 4
 CHUNK = SLOTS // CHUNKS
@@ -368,9 +369,7 @@
             mode = jnp.dot(left, focal, preferred_element_type=jnp.float32)
             for part in range(2):
                 for lane in range(HALF // 128):
-                    rows = pl.ds(
-                        (part * 2 + lane) * WIDE + first + i, RANK, stride=GROUPS * COLS
-                    )
+                    rows = pl.ds((part * 2 + lane) * WIDE + (first + i) * PITCH, RANK)
                     wide_ref[rows, :] = (
                         mode[part * RANK : (part + 1) * RANK, lane * 128 : (lane + 1) * 128] * scale
                     )
@@ -378,9 +377,13 @@
     for part in range(2):
         for lane in range(HALF // 128):
             at = (part * 2 + lane) * WIDE
-            out_ref[part, :, :, lane * 128 : (lane + 1) * 128] = (
-                wide_ref[at : at + WIDE, :].reshape(RANK, GROUPS * COLS, 128).astype(jnp.bfloat16)
-            )
+
+            def gather(k, carry):
+                rows = wide_ref[pl.ds(at + k, GROUPS * COLS, stride=PITCH), :]
+                out_ref[part, k, :, lane * 128 : (lane + 1) * 128] = rows.astype(jnp.bfloat16)
+                return carry
+
+            lax.fori_loop(0, RANK, gather, 0, unroll=16)
         copies.append(pltpu.make_async_copy(out_ref.at[part], out_hbm.at[part], out_sem.at[part]))
         copies[-1].start()
     for copy in copies:

time: 95.2 us -> 95.2 us (level)
  no operation moved by 1% of the time
where the time goes in v6:
time: 95.2 us; the launch traced here: 94.9 us
  blocking collectives  56.5 us (59%)
  Pallas kernels  14.5 us (15%)
  waiting for transfers between devices  12 us (13%)
  starting transfers between devices  10.6 us (11%)
    all_to_all x1, blocking collectives, local(): pieces = lax.all_to_all(across, AXES, 0, 0, tiled=True)  41.4 us
    all_to_all x1, blocking collectives, local(): lax.all_to_all(total.reshape(DEVICES, 4, 128), AXES, 0, 0, tiled=True)  15.1 us
    all_to_all x1, waiting for transfers between devices, local(): lax.all_to_all(gram.reshape(DEVICES, 4, 128), AXES, 0, 0, tiled=True)  12 us
    all_to_all x1, starting transfers between devices, local(): lax.all_to_all(gram.reshape(DEVICES, 4, 128), AXES, 0, 0, tiled=True)  6.11 us
    pallas_call x1, Pallas kernels, local(): pl.pallas_call(spectra_kernel, out_shape=jax.ShapeDtypeStruct((DEVICES, C...  5.93 us
    pallas_call x1, Pallas kernels, local(): pl.pallas_call(focal_kernel, out_shape=(focal_shape(2 * COLS), focal_shap...  3.71 us
    ppermute x1, starting transfers between devices, local(): swap_first = lax.ppermute(swap_first, 'grp', [(0, 1), (1, 0)])  3.33 us
    pallas_call x1, Pallas kernels, local(): pl.pallas_call(power_kernel, out_shape=(jax.ShapeDtypeStruct((2 * RANK, 2...  2.94 us
  transfers between devices with their start and end apart: 3, of which 1 were waited for; matrix products, arithmetic and copies ran while one was open for 0% of the time, Pallas kernels for 3%

profile of v6, /device:TPU:1, one launch (start us, length us, event | category | flops | bytes accessed | tf_op | source)
XLA Modules:
  0.0 94.9 jit_solution(4961430930721472999)
XLA Ops:
  0.6 5.9 %spectra.1 = bf16[128,4,16,128]{3,2,1,0:T(8,128)(2,1)S(1)} custom-call(s32[1]{0:T(128)} %bitcast.group_ref, s32[256]{0:T(256)} %assign_hbm.1, f32[256]{0:T(256)} %occ_hbm.1, f32[256]{0:T(256)} %chrom_hbm.1, bf16[2,128,8,512]{3,2,1,0:T(8,128)(2,1)} %bitcast.12, f32[8,512]{1,0:T(8,128)} %lens_hbm.1, bf16[2,512,512]{2,1,0:T(8,128)(2,1)} %constant.10.clone.table_hbm), custom_call_target="tpu_custom_call" | custom-call | tf_op jit(solution)/shard_map/spectra/pallas_call | solution.py:405
  6.6 0.0 copy-start
  6.6 41.4 %all_to_all.15 = bf16[128,4,16,128]{3,2,1,0:T(8,128)(2,1)S(1)} all-to-all(bf16[128,4,16,128]{3,2,1,0:T(8,128)(2,1)S(1)} %spectra.1), channel_id=1, replica_groups=mesh['grp'=2,'pix'=64] {'grp','pix'}, dimensions={0} | all-to-all | bytes 4194304 | tf_op jit(solution)/shard_map/all_to_all | solution.py:436
  48.0 0.0 copy-done
  48.0 0.0 copy-start.1
  48.0 3.7 %focal.1 = (bf16[8,256,256]{2,1,0:T(8,128)(2,1)S(1)}, bf16[3,256,256]{2,1,0:T(8,128)(2,1)S(1)}, bf16[5,256,256]{2,1,0:T(8,128)(2,1)S(1)}, f32[512,128]{1,0:T(8,128)}) custom-call(s32[1]{0:T(128)} %bitcast.group_ref, bf16[128,4,2,8,128]{4,3,2,1,0:T(8,128)(2,1)S(1)} %bitcast.8, bf16[2,512,512]{2,1,0:T(8,128)(2,1)S(1)} %copy-done), custom_call_target="tpu_custom_call" | custom-call | tf_op jit(solution)/shard_map/focal/pallas_call | solution.py:443
  51.7 0.0 copy-start.2
  51.7 0.7 copy-done.2
  52.4 1.1 %collective-permute-start.1 = (bf16[5,256,256]{2,1,0:T(8,128)(2,1)S(1)}, bf16[5,256,256]{2,1,0:T(8,128)(2,1)S(1)}, u32[]{:S(2)}, u32[]{:S(2)}) collective-permute-start(bf16[5,256,256]{2,1,0:T(8,128)(2,1)S(1)} %get-tuple-element.14), channel_id=1, source_target_pairs={{0,64},{64,0},{1,65},{65,1},{2,66},{66,2},{3,67},{67,3},{4,68},{68... | collective-permute-start | bytes 1966088 | tf_op jit(solution)/shard_map/ppermute | solution.py:457
  53.6 6.1 %all-to-all-start.1 = ((f32[128,4,128]{2,1,0:T(4,128)}), f32[128,4,128]{2,1,0:T(4,128)S(1)}, u32[]{:S(2)}, u32[]{:S(2)}) async-start(f32[128,4,128]{2,1,0:T(4,128)} %bitcast.3), calls=%async_computation.1 | async-start | bytes 524288 | tf_op jit(solution)/shard_map/all_to_all | solution.py:458
  59.7 3.3 %collective-permute-start = (bf16[3,256,256]{2,1,0:T(8,128)(2,1)}, bf16[3,256,256]{2,1,0:T(8,128)(2,1)S(1)}, u32[]{:S(2)}, u32[]{:S(2)}) collective-permute-start(bf16[3,256,256]{2,1,0:T(8,128)(2,1)} %copy-done.2), channel_id=1, source_target_pairs={{0,64},{64,0},{1,65},{65,1},{2,66},{66,2},{3,67},{67,3},{4,68},{68... | collective-permute-start | bytes 1179656 | tf_op jit(solution)/shard_map/ppermute | solution.py:456
  63.0 12.0 %all-to-all-done.1 = f32[128,4,128]{2,1,0:T(4,128)S(1)} async-done(((f32[128,4,128]{2,1,0:T(4,128)}), f32[128,4,128]{2,1,0:T(4,128)S(1)}, u32[]{:S(2)}, u32[]{:S(2)}) %all-to-all-start.1) | async-done | bytes 262176 | tf_op jit(solution)/shard_map/all_to_all | solution.py:458
  75.0 0.1 total.1
  75.1 15.1 %all_to_all.16 = f32[128,4,128]{2,1,0:T(4,128)S(1)} all-to-all(f32[128,4,128]{2,1,0:T(4,128)S(1)} %bitcast.11), channel_id=1, replica_groups=mesh['grp'=2,'pix'=64] {'grp','pix'}, dimensions={0} | all-to-all | bytes 524288 | tf_op jit(solution)/shard_map/all_to_all | solution.py:467
  90.2 0.0 copy-done.1
  90.2 2.9 %power.1 = (bf16[256,512]{1,0:T(8,128)(2,1)S(1)}, f32[128,128]{1,0:T(8,128)S(1)}, f32[1,128]{1,0:T(1,128)}) custom-call(f32[512,128]{1,0:T(8,128)S(1)} %bitcast.10, f32[2,256,128]{2,1,0:T(8,128)S(1)} %copy-done.1), custom_call_target="tpu_custom_call" | custom-call | tf_op jit(solution)/shard_map/power/pallas_call | solution.py:468
  93.1 0.0 collective-permute-done.first_ref
  93.1 0.0 collective-permute-done.1.second_ref
  93.1 1.8 %modes.1 = bf16[2,128,8,256]{3,2,1,0:T(8,128)(2,1)} custom-call(s32[1]{0:T(128)} %bitcast.group_ref, bf16[256,512]{1,0:T(8,128)(2,1)S(1)} %get-tuple-element.10.left_ref, f32[128,128]{1,0:T(8,128)S(1)} %get-tuple-element.11.scale_ref, bf16[8,256,256]{2,1,0:T(8,128)(2,1)S(1)} %get-tuple-element.12.kept_ref, ...), custom_call_target="tpu_custom_call" | custom-call | tf_op jit(solution)/shard_map/modes/pallas_call | solution.py:480
Async XLA Ops:
  6.6 41.4 %copy-start = (bf16[2,512,512]{2,1,0:T(8,128)(2,1)S(1)}, bf16[2,512,512]{2,1,0:T(8,128)(2,1)}, u32[]{:S(2)}) copy-start(bf16[2,512,512]{2,1,0:T(8,128)(2,1)} %constant.11.clone.table_ref) | copy-start | bytes 3145732
  48.0 42.2 %copy-start.1 = (f32[2,256,128]{2,1,0:T(8,128)S(1)}, f32[2,256,128]{2,1,0:T(8,128)}, u32[]{:S(2)}) copy-start(f32[2,256,128]{2,1,0:T(8,128)} %start_ref.1) | copy-start | bytes 786436
  51.7 0.7 copy-start.2
  52.4 40.7 %collective-permute-start.1 = (bf16[5,256,256]{2,1,0:T(8,128)(2,1)S(1)}, bf16[5,256,256]{2,1,0:T(8,128)(2,1)S(1)}, u32[]{:S(2)}, u32[]{:S(2)}) collective-permute-start(bf16[5,256,256]{2,1,0:T(8,128)(2,1)S(1)} %get-tuple-element.14), channel_id=1, source_target_pairs={{0,64},{64,0},{1,65},{65,1},{2,66},{66,2},{3,67},{67,3},{4,68},{68... | collective-permute-start | bytes 1966088 | tf_op jit(solution)/shard_map/ppermute | solution.py:457
  53.6 21.4 %all-to-all-start.1 = ((f32[128,4,128]{2,1,0:T(4,128)}), f32[128,4,128]{2,1,0:T(4,128)S(1)}, u32[]{:S(2)}, u32[]{:S(2)}) async-start(f32[128,4,128]{2,1,0:T(4,128)} %bitcast.3), calls=%async_computation.1 | async-start | bytes 524288 | tf_op jit(solution)/shard_map/all_to_all | solution.py:458
  59.7 33.4 %collective-permute-start = (bf16[3,256,256]{2,1,0:T(8,128)(2,1)}, bf16[3,256,256]{2,1,0:T(8,128)(2,1)S(1)}, u32[]{:S(2)}, u32[]{:S(2)}) collective-permute-start(bf16[3,256,256]{2,1,0:T(8,128)(2,1)} %copy-done.2), channel_id=1, source_target_pairs={{0,64},{64,0},{1,65},{65,1},{2,66},{66,2},{3,67},{67,3},{4,68},{68... | collective-permute-start | bytes 1179656 | tf_op jit(solution)/shard_map/ppermute | solution.py:456
